TPU v7x, 32 devices: a whole 2x2x4 slice. The times are simulated.
32 devices in a mesh: grp: 2 (over x), seq: 8 (over z, y), ch: 2 (over core).
Axes of the slice: x: 2, y: 2, z: 4, core: 2. Of those that a mesh axis runs over, the one named last changes fastest.
Arguments:
- seq_in: bfloat16 [4096, 1536], P(('grp', 'seq'), 'ch'), parts along dimension 0, may hold values from -6 to 6
- conv_gain: float32 [2, 1536], P(None, 'ch'), may hold values from 0.5 to 1.5
- dw_kernel: float32 [2, 5, 1536], P(None, None, 'ch'), may hold values from -2.5 to 2.5
- mix_weight: bfloat16 [2, 1536, 1536], P(None, 'ch'), may hold values from -0.15625 to 0.15625
- attn_gain: float32 [1536], P('ch'), may hold values from 0.8 to 100, as said below
- q_weight: bfloat16 [1536, 1024], P(None, 'ch'), may hold values from -0.15625 to 0.15625
- kv_weight: bfloat16 [1536, 2, 256], P(None, None, 'ch'), may hold values from -0.15625 to 0.15625
- out_weight: bfloat16 [1024, 1536], P('ch'), may hold values from -0.1875 to 0.1875
Outputs:
- seq_out: bfloat16 [4096, 1536], P(('grp', 'seq'), 'ch'), parts along dimension 0
There are 2 independent parts, one for each index of `grp`. A program takes and returns all parts, laid end to end along the dimension named above; an argument that names none is the same for every part. Nothing has to cross between parts.
Inputs may be any that keep to these rules, and one draw needn't show every extreme that they name: `attn_gain`: gains of the attention norm are positive.
All inputs are finite; a program needn't handle non-finite values.
Results may differ from a plain program's by a relative error of at most 0.03.
The roundings to bfloat16 on the way count: a program that leaves them out, or rounds other values in their place, can miss the bound.
Values may be sent and summed in bfloat16 or wider, within the bound.
No kernel may reach another device: no remote copies, remote signals or barrier semaphores. Data moves between devices by JAX's collectives and lax.ppermute only.
A program may use at most 64 MiB of HBM per device.

v0:
```python
import math

import jax
import jax.numpy as jnp
from jax import lax
from jax.sharding import PartitionSpec as P

HD = 128


EPSILON = 1e-06


def extended(shard, sides, width):
    for axis, dim in sides:
        size, length = (lax.axis_size(axis), shard.shape[dim])
        up = [(i, (i + 1) % size) for i in range(size - 1)]
        down = [(j, i) for i, j in up]
        last = lax.slice_in_dim(shard, length - width, length, axis=dim)
        initial = lax.slice_in_dim(shard, 0, width, axis=dim)
        before = lax.ppermute(last, axis, up)
        after = lax.ppermute(initial, axis, down)
        shard = jnp.concatenate([before, shard, after], axis=dim)
    return shard


def row_normalize(hidden, gain):
    channels = hidden.shape[1] * lax.axis_size("ch")
    squares = lax.psum(jnp.sum(hidden * hidden, axis=1), "ch")
    return hidden * lax.rsqrt(squares[:, None] / channels + EPSILON) * gain


def dilated_sum(padded, kernels, dilation, row_count):
    summed = padded[0:row_count] * kernels[0]
    for tap_index in range(1, kernels.shape[0]):
        summed = (
            summed
            + padded[tap_index * dilation : tap_index * dilation + row_count] * kernels[tap_index]
        )
    return summed


def channel_mix(gelu_output, weight):
    return lax.psum_scatter(
        jnp.dot(gelu_output, weight, preferred_element_type=jnp.float32),
        "ch",
        scatter_dimension=1,
        tiled=True,
    )


def local(seq_in, conv_gain, dw_kernel, mix_weight, attn_gain, q_weight, kv_weight, out_weight):
    local_rows = seq_in.shape[0]
    kernel_half = dw_kernel.shape[1] // 2
    dilation_list = [local_rows // 8, local_rows // 4]
    first_reach = kernel_half * dilation_list[0]
    second_reach = kernel_half * dilation_list[1]
    widened = extended(seq_in, (("seq", 0),), first_reach + second_reach).astype(jnp.float32)
    normalized_rows = row_normalize(widened, conv_gain[0])
    leading_rows = local_rows + 2 * second_reach
    summed = dilated_sum(normalized_rows, dw_kernel[0], dilation_list[0], leading_rows)
    gelu_output = jax.nn.gelu(summed, approximate=True).astype(jnp.bfloat16)
    middle = widened[first_reach : first_reach + leading_rows] + channel_mix(
        gelu_output, mix_weight[0]
    )
    position = (
        lax.axis_index("seq") * local_rows
        - second_reach
        + lax.broadcasted_iota(jnp.int32, (leading_rows,), 0)
    )
    inside = (position >= 0) & (position < local_rows * lax.axis_size("seq"))
    middle = jnp.where(inside[:, None], middle, 0.0)
    normalized_rows = row_normalize(middle, conv_gain[1])
    summed = dilated_sum(normalized_rows, dw_kernel[1], dilation_list[1], local_rows)
    gelu_output = jax.nn.gelu(summed, approximate=True).astype(jnp.bfloat16)
    hidden = middle[second_reach : second_reach + local_rows] + channel_mix(
        gelu_output, mix_weight[1]
    )
    normalized_rows = row_normalize(hidden, attn_gain).astype(jnp.bfloat16)
    features = lax.all_gather(normalized_rows, "ch", axis=1, tiled=True)
    query_rows = jnp.dot(features, q_weight, preferred_element_type=jnp.float32).astype(
        jnp.bfloat16
    )
    kv_width = kv_weight.shape[2]
    pairs = jnp.dot(
        features,
        kv_weight.reshape(kv_weight.shape[0], 2 * kv_width),
        preferred_element_type=jnp.float32,
    ).astype(jnp.bfloat16)
    keys_local = pairs[:, :kv_width]
    values_local = pairs[:, kv_width:]
    kv_local = kv_width // HD
    group_size = q_weight.shape[1] // HD // kv_local
    query_grid = query_rows.reshape(local_rows, kv_local, group_size, HD)
    scale = 1.0 / math.sqrt(HD)

    def key_block(carry, block):
        running_max, running_sum, context = carry
        key_part, value_part = block
        scores = (
            jnp.einsum("pkgd,skd->kgps", query_grid, key_part, preferred_element_type=jnp.float32)
            * scale
        )
        new_max = jnp.maximum(running_max, jnp.max(scores, axis=-1))
        factor = jnp.exp(running_max - new_max)
        probs = jnp.exp(scores - new_max[..., None])
        running_sum = running_sum * factor + jnp.sum(probs, axis=-1)
        update = jnp.einsum(
            "kgps,skd->kgpd",
            probs.astype(jnp.bfloat16),
            value_part,
            preferred_element_type=jnp.float32,
        )
        context = context * factor[..., None] + update
        return ((new_max, running_sum, context), None)

    initial = (
        jnp.full((kv_local, group_size, local_rows), -1e30, jnp.float32),
        jnp.zeros((kv_local, group_size, local_rows), jnp.float32),
        jnp.zeros((kv_local, group_size, local_rows, HD), jnp.float32),
    )
    carry = initial
    key_piece = lax.all_gather(keys_local, "seq", axis=0, tiled=True)
    value_piece = lax.all_gather(values_local, "seq", axis=0, tiled=True)
    key_count = key_piece.shape[0]
    block_len = math.gcd(key_count, 512)
    blocks = (
        key_piece.reshape(key_count // block_len, block_len, kv_local, HD),
        value_piece.reshape(key_count // block_len, block_len, kv_local, HD),
    )
    carry, unused = lax.scan(key_block, carry, blocks)
    running_max, running_sum, context = carry
    attended = (context / running_sum[..., None]).astype(jnp.bfloat16)
    attended = jnp.transpose(attended, (2, 0, 1, 3)).reshape(local_rows, kv_local * group_size * HD)
    mixed = lax.psum_scatter(
        jnp.dot(attended, out_weight, preferred_element_type=jnp.float32).astype(jnp.bfloat16),
        "ch",
        scatter_dimension=1,
        tiled=True,
    ).astype(jnp.float32)
    return (hidden + mixed).astype(jnp.bfloat16)


def solution(mesh):
    return jax.shard_map(
        local,
        mesh=mesh,
        in_specs=(
            P(("grp", "seq"), "ch"),
            P(None, "ch"),
            P(None, None, "ch"),
            P(None, "ch", None),
            P("ch"),
            P(None, "ch"),
            P(None, None, "ch"),
            P("ch", None),
        ),
        out_specs=P(("grp", "seq"), "ch"),
        check_vma=False,
    )
```

profile of v0, /device:TPU:0, one launch (start us, length us, event | category | flops | bytes accessed | tf_op | source)
XLA Modules:
  0.0 192.6 jit_solution(12931244962817168558)
XLA Ops:
  7.8 4.9 %collective-permute-start = (bf16[192,768]{1,0:T(8,128)(2,1)S(1)}, bf16[192,768]{1,0:T(8,128)(2,1)S(1)}, u32[]{:S(2)}, u32[]{:S(2)}) collective-permute-start(bf16[192,768]{1,0:T(8,128)(2,1)S(1)} %get-tuple-element.115), channel_id=1, source_target_pairs={{0,2},{2,4},{4,6},{6,8},{8,10},{10,12},{12,14},{1,3},{3,5},{5,7},{... | collective-permute-start | bytes 884744 | tf_op jit(solution)/shard_map/ppermute | solution.py:21
  15.7 9.5 %collective-permute-done = bf16[192,768]{1,0:T(8,128)(2,1)S(1)} collective-permute-done((bf16[192,768]{1,0:T(8,128)(2,1)S(1)}, bf16[192,768]{1,0:T(8,128)(2,1)S(1)}, u32[]{:S(2)}, u32[]{:S(2)}) %collective-permute-start) | collective-permute-done | bytes 294944 | tf_op jit(solution)/shard_map/ppermute | solution.py:21
  26.5 2.5 %psum.21 = f32[640]{0:T(1024)S(1)} all-reduce(f32[640]{0:T(1024)S(1)} %multiply_reduce_fusion), channel_id=1, replica_groups=mesh['grp'=2,'seq'=8,'ch'=2] {'ch'}, use_global_device_ids=true, to_apply=%region_1.0 | all-reduce | flops 640 | bytes 5120 | tf_op jit(solution)/shard_map/psum | solution.py:29
  29.2 5.3 %fusion.20 = f32[512,1536]{1,0:T(8,128)} fusion(bf16[2,768,1536]{2,1,0:T(8,128)(2,1)} %param.13, f32[640,768]{1,0:T(8,128)S(1)} %multiply_multiply_fusion.1, f32[768]{0:T(1024)S(1)} %get-tuple-element.86, f32[768]{0:T(1024)S(1)} %get-tuple-element.87, f32[768]{0:T(1024)S(1)} %get-tuple-element.88, f32[768]{0:T(1024)S(1)} %get-tuple-element.89, ...), kind=kOutput, calls=%fused_computation.29 | convolution fusion | flops 1215037440 | bytes 13389824 | tf_op jit(solution)/shard_map/dot_general | solution.py:45
  36.1 11.7 %reduce-scatter.4.cloned.1.call-done = f32[512,768]{1,0:T(8,128)} async-done(((f32[512,1536]{1,0:T(8,128)}), f32[512,768]{1,0:T(8,128)}) %reduce-scatter.4.cloned.1.call-update) | async-done | bytes 1572880 | tf_op jit(solution)/shard_map/reduce_scatter | solution.py:44
  47.8 2.2 %multiply_reduce_fusion.1 = (f32[512]{0:T(512)S(1)}, f32[512,768]{1,0:T(8,128)S(1)}) fusion(f32[512,768]{1,0:T(8,128)} %reduce-scatter.4.cloned.1.call-done, f32[640,768]{1,0:T(8,128)} %maximum_convert_fusion, pred[512]{0:T(512)(128)(4,1)S(1)} %fusion.73), kind=kLoop, calls=%fused_computation.55 | loop fusion | flops 1572352 | bytes 4721152 | tf_op jit(solution)/shard_map/reduce_sum | solution.py:29
  50.0 2.5 %psum.22 = f32[512]{0:T(512)S(1)} all-reduce(f32[512]{0:T(512)S(1)} %get-tuple-element.111), channel_id=1, replica_groups=mesh['grp'=2,'seq'=8,'ch'=2] {'ch'}, use_global_device_ids=true, to_apply=%region_4.5 | all-reduce | flops 512 | bytes 4096 | tf_op jit(solution)/shard_map/psum | solution.py:29
  52.7 3.9 %fusion.18 = f32[256,1536]{1,0:T(8,128)} fusion(bf16[2,768,1536]{2,1,0:T(8,128)(2,1)} %param.13, f32[512,768]{1,0:T(8,128)S(1)} %multiply_multiply_fusion.2, f32[768]{0:T(1024)S(1)} %get-tuple-element.91, f32[768]{0:T(1024)S(1)} %get-tuple-element.92, f32[768]{0:T(1024)S(1)} %get-tuple-element.84, f32[768]{0:T(1024)S(1)} %get-tuple-element.85, ...), kind=kOutput, calls=%fused_computation.27 | convolution fusion | flops 607518720 | bytes 7884800 | tf_op jit(solution)/shard_map/dot_general | solution.py:45
  56.7 10.3 %reduce-scatter.6.cloned.1.call-done = f32[256,768]{1,0:T(8,128)} async-done(((f32[256,1536]{1,0:T(8,128)}), f32[256,768]{1,0:T(8,128)}) %reduce-scatter.6.cloned.1.call-update) | async-done | bytes 786448 | tf_op jit(solution)/shard_map/reduce_scatter | solution.py:44
  68.3 2.5 %psum.23 = f32[256]{0:T(256)S(1)} all-reduce(f32[256]{0:T(256)S(1)} %multiply_reduce_fusion.2), channel_id=1, replica_groups=mesh['grp'=2,'seq'=8,'ch'=2] {'ch'}, use_global_device_ids=true, to_apply=%region_7.8 | all-reduce | flops 256 | bytes 2048 | tf_op jit(solution)/shard_map/psum | solution.py:29
  72.1 2.4 %all_gather.9 = bf16[256,1536]{1,0:T(8,128)(2,1)S(1)} all-gather(bf16[256,768]{1,0:T(8,128)(2,1)S(1)} %multiply_convert_fusion), channel_id=1, replica_groups=mesh['grp'=2,'seq'=8,'ch'=2] {'ch'}, dimensions={1}, use_global_device_ids=true | all-gather | bytes 1179648 | tf_op jit(solution)/shard_map/all_gather | solution.py:80
  74.9 33.7 %all_gather.10 = bf16[2048,128]{1,0:T(8,128)(2,1)} all-gather(bf16[256,128]{1,0:T(8,128)(2,1)S(1)} %get-tuple-element.118), channel_id=1, replica_groups=mesh['grp'=2,'seq'=8,'ch'=2] {'seq'}, dimensions={0}, use_global_device_ids=true | all-gather | bytes 589824 | tf_op jit(solution)/shard_map/all_gather | solution.py:123
  108.6 33.4 %all_gather.11 = bf16[2048,128]{1,0:T(8,128)(2,1)} all-gather(bf16[256,128]{1,0:T(8,128)(2,1)S(1)} %get-tuple-element.117), channel_id=1, replica_groups=mesh['grp'=2,'seq'=8,'ch'=2] {'seq'}, dimensions={0}, use_global_device_ids=true | all-gather | bytes 589824 | tf_op jit(solution)/shard_map/all_gather | solution.py:124
  144.3 25.2 %while.15 = (s32[]{:T(128)}, f32[1,4,256]{2,1,0:T(4,128)S(1)}, f32[1,4,256]{2,1,0:T(4,128)S(1)}, f32[1,4,256,128]{3,2,1,0:T(8,128)}, bf16[4,512,1,128]{3,1,2,0:T...) while((s32[]{:T(128)}, f32[1,4,256]{2,1,0:T(4,128)S(1)}, ...), condition=%wide.region_11.12_spmd.clone, body=%wide.region_8.11_spmd.clone.sunk | while | flops 273029120 | bytes 16319621 | solution.py:131
  144.3 2.7 %bitcast_reduce_fusion.2 = (f32[4,256]{1,0:T(4,128)S(1)}, f32[512,256,4]{1,0,2:T(8,128)}) fusion(bf16[256,1,4,128]{3,0,2,1:T(8,128)(2,1)S(1)} %get-tuple-element.193, bf16[4,512,1,128]{3,1,2,0:T(8,128)(2,1)} %get-tuple-element.192, s32[]{:T(128)} %get-tuple-element.179), kind=kOutput, calls=%fused_computation.1.clone.1 | convolution fusion | flops 135265280 | bytes 2494976 | tf_op jit(solution)/shard_map/while/body/eval_jaxpr/pkgd,skd->kgps/dot_general | solution.py:101
  147.1 3.1 %fusion.99 = f32[1,4,256,128]{3,2,1,0:T(8,128)} fusion(f32[512,256,4]{1,0,2:T(8,128)} %get-tuple-element.168, f32[4,256]{1,0:T(4,128)S(1)} %bitcast.95, f32[1,4,256,128]{3,2,1,0:T(8,128)} %get-tuple-element.182, f32[4,256]{1,0:T(4,128)S(1)} %get-tuple-element.169, pred[]{:T(512)S(6)} %compare.3, bf16[4,512,1,128]{3,1,2,0:T(8,128)(2,1)} %get-tuple-element.194, ...), kind=kOutput, calls=%fused_computation.6.clone.1 | convolution fusion | flops 136183808 | bytes 3285505 | tf_op jit(solution)/shard_map/while/body/eval_jaxpr/kgps,skd->kgpd/dot_general | solution.py:108
  150.5 2.7 %bitcast_reduce_fusion.2 = (f32[4,256]{1,0:T(4,128)S(1)}, f32[512,256,4]{1,0,2:T(8,128)}) fusion(bf16[256,1,4,128]{3,0,2,1:T(8,128)(2,1)S(1)} %get-tuple-element.193, bf16[4,512,1,128]{3,1,2,0:T(8,128)(2,1)} %get-tuple-element.192, s32[]{:T(128)} %get-tuple-element.179), kind=kOutput, calls=%fused_computation.1.clone.1 | convolution fusion | flops 135265280 | bytes 2494976 | tf_op jit(solution)/shard_map/while/body/eval_jaxpr/pkgd,skd->kgps/dot_general | solution.py:101
  153.3 3.2 %fusion.99 = f32[1,4,256,128]{3,2,1,0:T(8,128)} fusion(f32[512,256,4]{1,0,2:T(8,128)} %get-tuple-element.168, f32[4,256]{1,0:T(4,128)S(1)} %bitcast.95, f32[1,4,256,128]{3,2,1,0:T(8,128)} %get-tuple-element.182, f32[4,256]{1,0:T(4,128)S(1)} %get-tuple-element.169, pred[]{:T(512)S(6)} %compare.3, bf16[4,512,1,128]{3,1,2,0:T(8,128)(2,1)} %get-tuple-element.194, ...), kind=kOutput, calls=%fused_computation.6.clone.1 | convolution fusion | flops 136183808 | bytes 3285505 | tf_op jit(solution)/shard_map/while/body/eval_jaxpr/kgps,skd->kgpd/dot_general | solution.py:108
  156.9 2.7 %bitcast_reduce_fusion.2 = (f32[4,256]{1,0:T(4,128)S(1)}, f32[512,256,4]{1,0,2:T(8,128)}) fusion(bf16[256,1,4,128]{3,0,2,1:T(8,128)(2,1)S(1)} %get-tuple-element.193, bf16[4,512,1,128]{3,1,2,0:T(8,128)(2,1)} %get-tuple-element.192, s32[]{:T(128)} %get-tuple-element.179), kind=kOutput, calls=%fused_computation.1.clone.1 | convolution fusion | flops 135265280 | bytes 2494976 | tf_op jit(solution)/shard_map/while/body/eval_jaxpr/pkgd,skd->kgps/dot_general | solution.py:101
  159.6 3.2 %fusion.99 = f32[1,4,256,128]{3,2,1,0:T(8,128)} fusion(f32[512,256,4]{1,0,2:T(8,128)} %get-tuple-element.168, f32[4,256]{1,0:T(4,128)S(1)} %bitcast.95, f32[1,4,256,128]{3,2,1,0:T(8,128)} %get-tuple-element.182, f32[4,256]{1,0:T(4,128)S(1)} %get-tuple-element.169, pred[]{:T(512)S(6)} %compare.3, bf16[4,512,1,128]{3,1,2,0:T(8,128)(2,1)} %get-tuple-element.194, ...), kind=kOutput, calls=%fused_computation.6.clone.1 | convolution fusion | flops 136183808 | bytes 3285505 | tf_op jit(solution)/shard_map/while/body/eval_jaxpr/kgps,skd->kgpd/dot_general | solution.py:108
  163.2 2.7 %bitcast_reduce_fusion.2 = (f32[4,256]{1,0:T(4,128)S(1)}, f32[512,256,4]{1,0,2:T(8,128)}) fusion(bf16[256,1,4,128]{3,0,2,1:T(8,128)(2,1)S(1)} %get-tuple-element.193, bf16[4,512,1,128]{3,1,2,0:T(8,128)(2,1)} %get-tuple-element.192, s32[]{:T(128)} %get-tuple-element.179), kind=kOutput, calls=%fused_computation.1.clone.1 | convolution fusion | flops 135265280 | bytes 2494976 | tf_op jit(solution)/shard_map/while/body/eval_jaxpr/pkgd,skd->kgps/dot_general | solution.py:101
  165.9 3.2 %fusion.99 = f32[1,4,256,128]{3,2,1,0:T(8,128)} fusion(f32[512,256,4]{1,0,2:T(8,128)} %get-tuple-element.168, f32[4,256]{1,0:T(4,128)S(1)} %bitcast.95, f32[1,4,256,128]{3,2,1,0:T(8,128)} %get-tuple-element.182, f32[4,256]{1,0:T(4,128)S(1)} %get-tuple-element.169, pred[]{:T(512)S(6)} %compare.3, bf16[4,512,1,128]{3,1,2,0:T(8,128)(2,1)} %get-tuple-element.194, ...), kind=kOutput, calls=%fused_computation.6.clone.1 | convolution fusion | flops 136183808 | bytes 3285505 | tf_op jit(solution)/shard_map/while/body/eval_jaxpr/kgps,skd->kgpd/dot_general | solution.py:108
  174.2 9.8 %reduce-scatter.8.cloned.1.call-done = bf16[256,768]{1,0:T(8,128)(2,1)} async-done(((bf16[256,1536]{1,0:T(8,128)(2,1)}), bf16[256,768]{1,0:T(8,128)(2,1)}) %reduce-scatter.8.cloned.1.call-update) | async-done | bytes 393232 | tf_op jit(solution)/shard_map/reduce_scatter | solution.py:135
  184.0 2.1 %add_convert_fusion = bf16[256,768]{1,0:T(8,128)(2,1)} fusion(bf16[256,768]{1,0:T(8,128)(2,1)} %reduce-scatter.8.cloned.1.call-done, f32[256,768]{1,0:T(8,128)} %reduce-scatter.6.cloned.1.call-done, f32[512,768]{1,0:T(8,128)S(1)} %get-tuple-element.112), kind=kLoop, calls=%fused_computation.80 | loop fusion | flops 786432 | bytes 2359296 | tf_op jit(solution)/shard_map/convert_element_type | solution.py:141
  (66 shorter events, 19.1 us)
Async XLA Ops:
  6.5 166.2 %copy-start = (bf16[512,1536]{1,0:T(8,128)(2,1)S(1)}, bf16[512,1536]{1,0:T(8,128)(2,1)}, u32[]{:S(2)}) copy-start(bf16[512,1536]{1,0:T(8,128)(2,1)} %param.17) | copy-start | bytes 4718596
  6.5 22.4 %copy-start.2 = (bf16[256,768]{1,0:T(8,128)(2,1)S(1)}, bf16[256,768]{1,0:T(8,128)(2,1)}, u32[]{:S(2)}) copy-start(bf16[256,768]{1,0:T(8,128)(2,1)} %param.10) | copy-start | bytes 1179652
  6.5 41.2 %reduce-scatter.4.cloned.1.call-start = ((), (), s32[]{:S(2)}) async-start(), calls=%async_computation.3 | async-start | bytes 4718592 | tf_op jit(solution)/shard_map/reduce_scatter | solution.py:44
  7.8 17.4 %collective-permute-start = (bf16[192,768]{1,0:T(8,128)(2,1)S(1)}, bf16[192,768]{1,0:T(8,128)(2,1)S(1)}, u32[]{:S(2)}, u32[]{:S(2)}) collective-permute-start(bf16[192,768]{1,0:T(8,128)(2,1)S(1)} %get-tuple-element.115), channel_id=1, source_target_pairs={{0,2},{2,4},{4,6},{6,8},{8,10},{10,12},{12,14},{1,3},{3,5},{5,7},{... | collective-permute-start | bytes 884744 | tf_op jit(solution)/shard_map/ppermute | solution.py:21
  12.7 12.6 %collective-permute-start.1 = (bf16[192,768]{1,0:T(8,128)(2,1)S(1)}, bf16[192,768]{1,0:T(8,128)(2,1)S(1)}, u32[]{:S(2)}, u32[]{:S(2)}) collective-permute-start(bf16[192,768]{1,0:T(8,128)(2,1)S(1)} %get-tuple-element.116), channel_id=1, source_target_pairs={{2,0},{4,2},{6,4},{8,6},{10,8},{12,10},{14,12},{3,1},{5,3},{7,5},{... | collective-permute-start | bytes 884744 | tf_op jit(solution)/shard_map/ppermute | solution.py:22
  34.6 32.4 %reduce-scatter.6.cloned.1.call-start = ((), (), s32[]{:S(2)}) async-start(), calls=%async_computation.4 | async-start | bytes 2359296 | tf_op jit(solution)/shard_map/reduce_scatter | solution.py:44
  56.6 14.2 %copy-start.3 = (f32[768]{0:T(1024)S(1)}, f32[768]{0:T(1024)}, u32[]{:S(2)}) copy-start(f32[768]{0:T(1024)} %param.14) | copy-start | bytes 9220
  56.6 127.4 %reduce-scatter.8.cloned.1.call-start = ((), (), s32[]{:S(2)}) async-start(), calls=%async_computation.5 | async-start | bytes 1179648 | tf_op jit(solution)/shard_map/reduce_scatter | solution.py:135
  70.8 3.7 %copy-start.5 = (bf16[1536,2,128]{2,1,0:T(2,128)(2,1)S(1)}, bf16[1536,2,128]{2,1,0:T(2,128)(2,1)}, u32[]{:S(2)}) copy-start(bf16[1536,2,128]{2,1,0:T(2,128)(2,1)} %param.16) | copy-start | bytes 2359300
  74.5 67.5 %copy-start.4 = (bf16[1536,512]{1,0:T(8,128)(2,1)S(1)}, bf16[1536,512]{1,0:T(8,128)(2,1)}, u32[]{:S(2)}) copy-start(bf16[1536,512]{1,0:T(8,128)(2,1)} %param.15) | copy-start | bytes 4718596
  147.0 3.1 %copy-start.1 = (f32[512,256,4]{1,0,2:T(8,128)S(1)}, f32[512,256,4]{1,0,2:T(8,128)}, u32[]{:S(2)}) copy-start(f32[512,256,4]{1,0,2:T(8,128)} %get-tuple-element.168) | copy-start | bytes 6291460 | tf_op jit(solution)/shard_map/while
  153.3 3.2 %copy-start.1 = (f32[512,256,4]{1,0,2:T(8,128)S(1)}, f32[512,256,4]{1,0,2:T(8,128)}, u32[]{:S(2)}) copy-start(f32[512,256,4]{1,0,2:T(8,128)} %get-tuple-element.168) | copy-start | bytes 6291460 | tf_op jit(solution)/shard_map/while
  159.6 3.2 %copy-start.1 = (f32[512,256,4]{1,0,2:T(8,128)S(1)}, f32[512,256,4]{1,0,2:T(8,128)}, u32[]{:S(2)}) copy-start(f32[512,256,4]{1,0,2:T(8,128)} %get-tuple-element.168) | copy-start | bytes 6291460 | tf_op jit(solution)/shard_map/while
  165.9 3.2 %copy-start.1 = (f32[512,256,4]{1,0,2:T(8,128)S(1)}, f32[512,256,4]{1,0,2:T(8,128)}, u32[]{:S(2)}) copy-start(f32[512,256,4]{1,0,2:T(8,128)} %get-tuple-element.168) | copy-start | bytes 6291460 | tf_op jit(solution)/shard_map/while
Sparse Core Ops, SparseCore 0:
  34.7 13.0 reduce-scatter.3
  56.7 10.2 reduce-scatter.5
  174.3 9.6 reduce-scatter.7
where the time goes:
time: 193 us
  blocking collectives  76.9 us (40%)
  waiting for transfers between devices  41.4 us (21%)
  matrix products  35.1 us (18%)
  between operations  13.2 us (7%)
  other arithmetic  12.8 us (7%)
  local copies, waits for them, and re-layouts  6.81 us (4%)
  starting transfers between devices  6.27 us (3%)
    all_gather x1, blocking collectives, local(): key_piece = lax.all_gather(keys_local, 'seq', axis=0, tiled=True)  33.7 us
    all_gather x1, blocking collectives, local(): value_piece = lax.all_gather(values_local, 'seq', axis=0, tiled=True)  33.4 us
    reduce_scatter x2, waiting for transfers between devices, channel_mix(): lax.psum_scatter(jnp.dot(gelu_output, weight, preferred_element_type=jnp....  22 us
    dot_general x4, matrix products, key_block(): jnp.einsum('kgps,skd->kgpd', probs.astype(jnp.bfloat16), value_part, pref...  12.7 us
    dot_general x4, matrix products, key_block(): jnp.einsum('pkgd,skd->kgps', query_grid, key_part, preferred_element_type...  10.8 us
    reduce_scatter x1, waiting for transfers between devices, local(): lax.psum_scatter(jnp.dot(attended, out_weight, preferred_element_type=jnp...  9.8 us
    ppermute x1, waiting for transfers between devices, extended(): before = lax.ppermute(last, axis, up)  9.54 us
    dot_general x2, matrix products, channel_mix(): jnp.dot(gelu_output, weight, preferred_element_type=jnp.float32)  9.19 us
  transfers between devices with their start and end apart: 5, of which 4 were waited for; matrix products, arithmetic and copies ran while one was open for 2% of the time, Pallas kernels for 0%

commit v1 on v0

v1 whole, which is shorter than its diff:
```python
import functools
import math

import jax
import jax.numpy as jnp
from jax import lax
from jax.experimental import pallas as pl
from jax.experimental.pallas import tpu as pltpu
from jax.sharding import PartitionSpec as P

HD = 128
EPSILON = 1e-06
BF16 = jnp.bfloat16
F32 = jnp.float32
SWAP = [(0, 1), (1, 0)]
VMEM = pl.BlockSpec(memory_space=pltpu.VMEM)
SMEM = pl.BlockSpec(memory_space=pltpu.SMEM)
ANY = pl.BlockSpec(memory_space=pl.ANY)


def peer(array):
    return lax.ppermute(array, "ch", SWAP)


def ring_order(count):
    width = 1
    while width * width * 4 <= count:
        width *= 2
    rows = count // width
    if width == 1 or rows * width != count:
        return list(range(count))
    order = [row * width for row in range(rows)]
    for step, row in enumerate(reversed(range(rows))):
        columns = range(1, width) if step % 2 == 0 else range(width - 1, 0, -1)
        order += [row * width + column for column in columns]
    return order


def tower_kernel(
    place, x_own, x_peer, near_own, near_peer, far_own, far_peer, small_own, small_peer, mix_own, mix_peer,
    features, hidden_own, hidden_peer,
    wide, normed, middle, act, small, weights, sems,
    *, rows, first, second, length, taps,
):
    own = place[0]
    other = 1 - own
    half_taps = taps // 2
    reach1 = half_taps * second
    reach = half_taps * first + reach1
    mine = rows // 2
    lead = mine + 2 * reach1
    span = mine + 2 * reach
    width = x_own.shape[1]
    channels = 2 * width

    copies = []
    for layer in range(2):
        for side, source in ((own, mix_own), (other, mix_peer)):
            copy = pltpu.make_async_copy(source.at[layer], weights.at[layer, side], sems.at[layer, 0 if source is mix_own else 1])
            copy.start()
            copies.append(copy)

    near_at = pl.multiple_of(place[2], 64)
    far_at = pl.multiple_of(place[3], 64)
    for side, body, near, far, params in (
        (own, x_own, near_own, far_own, small_own),
        (other, x_peer, near_peer, far_peer, small_peer),
    ):
        wide[side, pl.ds(reach, rows), :] = body[...]
        wide[side, pl.ds(near_at, reach), :] = near[...]
        wide[side, pl.ds(far_at, reach), :] = far[...]
        small[side] = params[...]

    shift = pl.multiple_of(own * mine, 64)
    start = place[1] + own * mine
    chunk = 64

    def scale_of(parts, first_position):
        squares = jnp.sum(parts[0] * parts[0], axis=1, keepdims=True) + jnp.sum(parts[1] * parts[1], axis=1, keepdims=True)
        scale = lax.rsqrt(squares / channels + EPSILON)
        if first_position is None:
            return scale
        position = first_position + lax.broadcasted_iota(jnp.int32, scale.shape, 0)
        return jnp.where((position >= 0) & (position < length), scale, 0.0)

    def norm0(i, carry):
        at = pl.multiple_of(i * chunk, chunk)
        parts = [wide[h, pl.ds(pl.multiple_of(shift + at, 64), chunk), :].astype(F32) for h in range(2)]
        scale = scale_of(parts, start - reach + at)
        for h in range(2):
            normed[h, pl.ds(at, chunk), :] = parts[h] * scale * small[h, 0:1, :]
        return carry

    lax.fori_loop(0, span // chunk, norm0, 0)

    def convolve(layer, count, dilation):
        block = 32
        strip = 256

        def body(i, carry):
            at = pl.multiple_of(i * block, block)
            for h in range(2):
                for column in range(0, width, strip):
                    cols = pl.ds(column, strip)
                    total = None
                    for tap in range(taps):
                        kernel = small[h, pl.ds(2 + layer * taps + tap, 1), cols]
                        term = normed[h, pl.ds(pl.multiple_of(at + tap * dilation, 32), block), cols] * kernel
                        total = term if total is None else total + term
                    act[h, pl.ds(at, block), cols] = jax.nn.gelu(total, approximate=True).astype(BF16)
            return carry

        lax.fori_loop(0, count // block, body, 0)

    convolve(0, lead, first)
    copies[0].wait()
    copies[1].wait()
    for h in range(2):
        cols = pl.ds(h * width, width)
        mixed = jnp.dot(act[0, 0:lead, :], weights[0, 0, :, cols], preferred_element_type=F32)
        mixed = mixed + jnp.dot(act[1, 0:lead, :], weights[0, 1, :, cols], preferred_element_type=F32)
        before = wide[h, pl.ds(pl.multiple_of(shift + reach - reach1, 32), lead), :].astype(F32)
        middle[h] = before + mixed

    def norm1(i, carry):
        at = pl.multiple_of(i * chunk, chunk)
        parts = [middle[h, pl.ds(at, chunk), :] for h in range(2)]
        scale = scale_of(parts, start - reach1 + at)
        for h in range(2):
            normed[h, pl.ds(at, chunk), :] = parts[h] * scale * small[h, 1:2, :]
        return carry

    lax.fori_loop(0, lead // chunk, norm1, 0)
    convolve(1, mine, second)
    copies[2].wait()
    copies[3].wait()
    parts = []
    for h in range(2):
        cols = pl.ds(h * width, width)
        mixed = jnp.dot(act[0, 0:mine, :], weights[1, 0, :, cols], preferred_element_type=F32)
        mixed = mixed + jnp.dot(act[1, 0:mine, :], weights[1, 1, :, cols], preferred_element_type=F32)
        middle[h, pl.ds(reach1, mine), :] = middle[h, pl.ds(reach1, mine), :] + mixed
    hidden_own[...] = middle[own, pl.ds(reach1, mine), :]
    hidden_peer[...] = middle[other, pl.ds(reach1, mine), :]
    parts = [middle[h, pl.ds(reach1, mine), :] for h in range(2)]
    scale = scale_of(parts, None)
    for h in range(2):
        features[:, h * width : (h + 1) * width] = (parts[h] * scale * small[h, pl.ds(2 + 2 * taps, 1), :]).astype(BF16)


def project_kernel(place, own_ref, peer_ref, weight, out):
    count = own_ref.shape[0]
    at = pl.multiple_of(place[0] * count, count)
    back = pl.multiple_of((1 - place[0]) * count, count)
    out[pl.ds(at, count), :] = jnp.dot(own_ref[...], weight[...], preferred_element_type=F32).astype(BF16)
    out[pl.ds(back, count), :] = jnp.dot(peer_ref[...], weight[...], preferred_element_type=F32).astype(BF16)


def attend_kernel(q_ref, *refs, scale):
    blocks, out = refs[:-1], refs[-1]
    factor = scale * math.log2(math.e)
    heads = q_ref.shape[1] // HD
    for head in range(heads):
        q = q_ref[:, head * HD : (head + 1) * HD]
        scores = [
            lax.dot_general(q, kv[:, 0:HD], (((1,), (1,)), ((), ())), preferred_element_type=F32) for kv in blocks
        ]
        peak = functools.reduce(jnp.maximum, [jnp.max(s, axis=1, keepdims=True) for s in scores])
        total = None
        context = None
        for s, kv in zip(scores, blocks):
            probs = jnp.exp2((s - peak) * factor)
            part = jnp.sum(probs, axis=1, keepdims=True)
            value = jnp.dot(probs.astype(BF16), kv[:, HD:], preferred_element_type=F32)
            total = part if total is None else total + part
            context = value if context is None else context + value
        out[:, head * HD : (head + 1) * HD] = (context / total).astype(BF16)


def finish_kernel(place, ctx_own, ctx_peer, w_own, w_peer, hid_own, hid_peer, out):
    count = hid_own.shape[0]
    width = hid_own.shape[1]
    cols = pl.ds(pl.multiple_of(place[0] * width, 128), width)
    for at, hid in ((place[0] * count, hid_own), ((1 - place[0]) * count, hid_peer)):
        rows = pl.ds(pl.multiple_of(at, count), count)
        mixed = jnp.dot(ctx_own[rows, :], w_own[:, cols], preferred_element_type=F32)
        mixed = mixed + jnp.dot(ctx_peer[rows, :], w_peer[...], preferred_element_type=F32)
        out[rows, :] = (hid[...] + mixed).astype(BF16)


def params(limit=100 << 20):
    return pltpu.CompilerParams(vmem_limit_bytes=56 << 20)


def local(seq_in, conv_gain, dw_kernel, mix_weight, attn_gain, q_weight, kv_weight, out_weight):
    rows, width = seq_in.shape
    taps = dw_kernel.shape[1]
    size = lax.axis_size("seq")
    me = lax.axis_index("seq")
    core = lax.axis_index("ch")
    first, second = rows // 8, rows // 4
    reach1 = taps // 2 * second
    reach = taps // 2 * first + reach1
    mine = rows // 2
    lead = mine + 2 * reach1
    span = mine + 2 * reach

    even = me % 2 == 0
    low, high = seq_in[:reach], seq_in[rows - reach :]
    near_pairs = [(i, i ^ 1) for i in range(size)]
    far_pairs = [(0, 0), (size - 1, size - 1)]
    for i in range(1, size - 1, 2):
        far_pairs += [(i, i + 1), (i + 1, i)]
    near = lax.ppermute(jnp.where(even, high, low), "seq", near_pairs)
    far = lax.ppermute(jnp.where(even, low, high), "seq", far_pairs)

    small = jnp.concatenate(
        [conv_gain, dw_kernel.reshape(2 * taps, width), attn_gain[None, :], jnp.zeros((3, width), F32)], axis=0
    )
    small_peer = peer(small)
    x_peer = peer(seq_in)
    mix_peer = peer(mix_weight)
    out_away = lax.dynamic_slice_in_dim(out_weight, (1 - core) * width, width, axis=1)
    out_peer = peer(out_away)
    near_peer = peer(near)
    far_peer = peer(far)

    bottom = rows + reach
    place = jnp.stack(
        [core, me * rows, jnp.where(even, bottom, 0), jnp.where(even, 0, bottom)]
    ).astype(jnp.int32)

    features, hidden_own, hidden_away = pl.pallas_call(
        functools.partial(
            tower_kernel, rows=rows, first=first, second=second, length=rows * size, taps=taps
        ),
        out_shape=(
            jax.ShapeDtypeStruct((mine, 2 * width), BF16),
            jax.ShapeDtypeStruct((mine, width), F32),
            jax.ShapeDtypeStruct((mine, width), F32),
        ),
        in_specs=[SMEM] + [VMEM] * 8 + [ANY] * 2,
        out_specs=(VMEM, VMEM, VMEM),
        scratch_shapes=[
            pltpu.VMEM((2, rows + 2 * reach, width), BF16),
            pltpu.VMEM((2, span, width), F32),
            pltpu.VMEM((2, lead, width), F32),
            pltpu.VMEM((2, lead, width), BF16),
            pltpu.VMEM((2,) + small.shape, F32),
            pltpu.VMEM((2, 2, width, 2 * width), BF16),
            pltpu.SemaphoreType.DMA((2, 2)),
        ],
        compiler_params=params(),
        name="tower",
    )(place, seq_in, x_peer, near, near_peer, far, far_peer, small, small_peer, mix_weight, mix_peer)

    features_peer = peer(features)
    kv_width = 2 * kv_weight.shape[2]

    def project(weight, name):
        return pl.pallas_call(
            project_kernel,
            out_shape=jax.ShapeDtypeStruct((rows, weight.shape[1]), BF16),
            in_specs=[SMEM, VMEM, VMEM, VMEM],
            out_specs=VMEM,
            compiler_params=params(),
            name=name,
        )(place, features, features_peer, weight)

    kv = project(kv_weight.reshape(2 * width, kv_width), "keyvalue")
    order = ring_order(size)
    ahead = [(order[i], order[(i + 1) % size]) for i in range(size)]
    behind = [(b, a) for a, b in ahead]
    blocks = [kv]
    up = down = kv
    for step in range(size // 2):
        up = lax.ppermute(up, "seq", ahead)
        blocks.append(up)
        if 2 * step + 2 < size:
            down = lax.ppermute(down, "seq", behind)
            blocks.append(down)
    hidden_peer = peer(hidden_away)
    queries = project(q_weight, "query")
    context = pl.pallas_call(
        functools.partial(attend_kernel, scale=1.0 / math.sqrt(HD)),
        out_shape=jax.ShapeDtypeStruct(queries.shape, BF16),
        in_specs=[VMEM] * (1 + len(blocks)),
        out_specs=VMEM,
        compiler_params=params(),
        name="attend",
    )(queries, *blocks)
    context_peer = peer(context)
    return pl.pallas_call(
        finish_kernel,
        out_shape=jax.ShapeDtypeStruct((rows, width), BF16),
        in_specs=[SMEM] + [VMEM] * 6,
        out_specs=VMEM,
        compiler_params=params(),
        name="finish",
    )(place, context, context_peer, out_weight, out_peer, hidden_own, hidden_peer)


def solution(mesh):
    return jax.shard_map(
        local,
        mesh=mesh,
        in_specs=(
            P(("grp", "seq"), "ch"),
            P(None, "ch"),
            P(None, None, "ch"),
            P(None, "ch", None),
            P("ch"),
            P(None, "ch"),
            P(None, None, "ch"),
            P("ch", None),
        ),
        out_specs=P(("grp", "seq"), "ch"),
        check_vma=False,
    )
```

time: 193 us -> 70.4 us (0.36)
  blocking collectives: 76.9 us -> 0 us
  matrix products: 35.1 us -> 0 us
  Pallas kernels: 0 us -> 23.8 us
  waiting for transfers between devices: 41.4 us -> 22.6 us
  between operations: 13.2 us -> 0.18 us
  other arithmetic: 12.8 us -> 2.5 us
  starting transfers between devices: 6.27 us -> 14.7 us
    all_gather x3 -> x0, blocking collectives: 69.5 us -> none  [the longest x1 33.7 us: local(): key_piece = lax.all_gather(keys_local, 'seq', axis=0, tiled=True)]
    dot_general x13 -> x0, matrix products: 35.1 us -> none  [the longest x4 12.7 us: key_block(): jnp.einsum('kgps,skd->kgpd', probs.astype(jnp.bfloat16), value_part, pref...]
    reduce_scatter x3 -> x0, waiting for transfers between devices: 31.8 us -> none  [the longest x2 22 us: channel_mix(): lax.psum_scatter(jnp.dot(gelu_output, weight, preferred_element_type=jnp....]
    pallas_call x0 -> x5, Pallas kernels: none -> 23.8 us  [the longest x1 9.68 us: local(): pl.pallas_call(functools.partial(tower_kernel, rows=rows, first=first, se...]
    ppermute x2 -> x18, waiting for transfers between devices: 9.54 us -> 22.6 us  [the longest x1 10.8 us: local(): near = lax.ppermute(jnp.where(even, high, low), 'seq', near_pairs)]
    ppermute x2 -> x18, starting transfers between devices: 6.18 us -> 14.7 us  [the longest x4 7.93 us: local(): up = lax.ppermute(up, 'seq', ahead)]
    psum x3 -> x0, blocking collectives: 7.4 us -> none  [row_normalize(): squares = lax.psum(jnp.sum(hidden * hidden, axis=1), 'ch')]
    reduce_sum x7 -> x0, other arithmetic: 6.23 us -> none  [the longest x3 4.79 us: row_normalize(): squares = lax.psum(jnp.sum(hidden * hidden, axis=1), 'ch')]
  transfers between devices with their start and end apart: 5 -> 18, of which waited for: 4 -> 9; matrix products, arithmetic and copies ran while one was open for 2% -> 7% of each run, Pallas kernels for 0% -> 12%
where the time goes in v1:
time: 70.4 us; the launch traced here: 70 us
  Pallas kernels  23.8 us (34%)
  waiting for transfers between devices  22.6 us (32%)
  starting transfers between devices  14.7 us (21%)
  local copies, waits for them, and re-layouts  6.22 us (9%)
  other arithmetic  2.5 us (4%)
    ppermute x1, waiting for transfers between devices, local(): near = lax.ppermute(jnp.where(even, high, low), 'seq', near_pairs)  10.8 us
    pallas_call x1, Pallas kernels, local(): pl.pallas_call(functools.partial(tower_kernel, rows=rows, first=first, se...  9.68 us
    ppermute x4, waiting for transfers between devices, local(): up = lax.ppermute(up, 'seq', ahead)  8.57 us
    ppermute x4, starting transfers between devices, local(): up = lax.ppermute(up, 'seq', ahead)  7.93 us
    pallas_call x1, Pallas kernels, local(): pl.pallas_call(functools.partial(attend_kernel, scale=1.0 / math.sqrt(HD)...  5.43 us
    pallas_call x2, Pallas kernels, project(): pl.pallas_call(project_kernel, out_shape=jax.ShapeDtypeStruct((rows, weig...  5.41 us
    unnamed x46, local copies, waits for them, and re-layouts  5.39 us
    pallas_call x1, Pallas kernels, local(): pl.pallas_call(finish_kernel, out_shape=jax.ShapeDtypeStruct((rows, width...  3.32 us
  transfers between devices with their start and end apart: 18, of which 9 were waited for; matrix products, arithmetic and copies ran while one was open for 7% of the time, Pallas kernels for 12%

profile of v1, /device:TPU:0, one launch (start us, length us, event | category | flops | bytes accessed | tf_op | source)
XLA Modules:
  0.0 70.0 jit_solution(8388620880234967220)
XLA Ops:
  0.5 1.1 %broadcast_select_fusion = (bf16[192,768]{1,0:T(8,128)(2,1)S(1)}, bf16[192,768]{1,0:T(8,128)(2,1)S(1)}) fusion(pred[]{:T(512)S(6)} %eq.5, bf16[256,768]{1,0:T(8,128)(2,1)} %x_own.1), kind=kLoop, calls=%fused_computation.1 | loop fusion | flops 294912 | bytes 1179649 | tf_op jit(solution)/shard_map/jit(_where)/select_n | solution.py:215
  1.5 2.6 %collective-permute-start.1 = (bf16[192,768]{1,0:T(8,128)(2,1)S(1)}, bf16[192,768]{1,0:T(8,128)(2,1)S(1)}, u32[]{:S(2)}, u32[]{:S(2)}) collective-permute-start(bf16[192,768]{1,0:T(8,128)(2,1)S(1)} %get-tuple-element.12), channel_id=1, source_target_pairs={{0,2},{2,0},{4,6},{6,4},{8,10},{10,8},{12,14},{14,12},{1,3},{3,1},... | collective-permute-start | bytes 884744 | tf_op jit(solution)/shard_map/ppermute | solution.py:214
  5.1 0.8 %copy.10 = f32[2,5,768]{2,1,0:T(8,128)S(1)} copy(f32[2,5,768]{2,0,1:T(2,128)} %param.10) | data formatting | bytes 61440 | tf_op args[2]
  5.9 0.7 broadcast_in_dim.6
  6.6 10.8 %collective-permute-done.1.near_own = bf16[192,768]{1,0:T(8,128)(2,1)S(1)} collective-permute-done((bf16[192,768]{1,0:T(8,128)(2,1)S(1)}, bf16[192,768]{1,0:T(8,128)(2,1)S(1)}, u32[]{:S(2)}, u32[]{:S(2)}) %collective-permute-start.1) | collective-permute-done | bytes 294944 | tf_op jit(solution)/shard_map/ppermute | solution.py:214
  17.9 0.8 %maximum_maximum_fusion.small_own = f32[16,768]{1,0:T(8,128)S(1)} fusion(f32[1,768]{1,0:T(1,128)S(1)} %broadcast_in_dim.6, f32[10,768]{1,0:T(8,128)S(1)} %reshape.6, f32[2,768]{1,0:T(2,128)} %param.9, f32[16]{0:T(128)S(1)} %pad.3.clone), kind=kLoop, calls=%fused_computation.3 | loop fusion | flops 36864 | bytes 89152 | tf_op jit(solution)/shard_map/concatenate | solution.py:217
  20.9 9.7 %tower.1 = (bf16[128,1536]{1,0:T(8,128)(2,1)}, f32[128,768]{1,0:T(8,128)}, f32[128,768]{1,0:T(8,128)}) custom-call(s32[4]{0:T(128)} %pad_add_fusion.place, bf16[256,768]{1,0:T(8,128)(2,1)} %x_own.1, bf16[256,768]{1,0:T(8,128)(2,1)} %copy-done.5, bf16[192,768]{1,0:T(8,128)(2,1)} %copy-done.7, bf16[192,768]{1,0:T(8,128)(2,1)} %copy-done.9, ...), custom_call_target="tpu_custom_call" | custom-call | tf_op jit(solution)/shard_map/tower/pallas_call | solution.py:233
  30.8 1.0 %copy.13 = bf16[192,8,2,128]{3,1,2,0:T(8,128)(2,1)} copy(bf16[192,8,2,128]{3,2,1,0:T(2,128)(2,1)S(1)} %bitcast.9) | data formatting | bytes 1572864
  31.8 0.8 %collective-permute-done.7.peer_ref = bf16[128,1536]{1,0:T(8,128)(2,1)S(1)} collective-permute-done((bf16[128,1536]{1,0:T(8,128)(2,1)}, bf16[128,1536]{1,0:T(8,128)(2,1)S(1)}, u32[]{:S(2)}, u32[]{:S(2)}) %collective-permute-start.7) | collective-permute-done | bytes 393248 | tf_op jit(solution)/shard_map/ppermute | solution.py:22
  32.6 0.7 %copy-done.1 = bf16[128,1536]{1,0:T(8,128)(2,1)} copy-done((bf16[128,1536]{1,0:T(8,128)(2,1)}, bf16[128,1536]{1,0:T(8,128)(2,1)S(1)}, u32[]{:S(2)}) %copy-start.1) | copy-done | bytes 393240
  33.3 2.5 %keyvalue.1.refs_0_ = bf16[256,256]{1,0:T(8,128)(2,1)} custom-call(s32[4]{0:T(128)} %pad_add_fusion.place, bf16[128,1536]{1,0:T(8,128)(2,1)} %get-tuple-element.8.own_ref, bf16[128,1536]{1,0:T(8,128)(2,1)} %copy-done.1, bf16[1536,256]{1,0:T(8,128)(2,1)} %bitcast.8), custom_call_target="tpu_custom_call" | custom-call | tf_op jit(solution)/shard_map/keyvalue/pallas_call | solution.py:261
  35.8 2.5 %collective-permute-start.8 = (bf16[256,256]{1,0:T(8,128)(2,1)}, bf16[256,256]{1,0:T(8,128)(2,1)S(1)}, u32[]{:S(2)}, u32[]{:S(2)}) collective-permute-start(bf16[256,256]{1,0:T(8,128)(2,1)} %keyvalue.1.refs_0_), channel_id=1, source_target_pairs={{0,4},{4,8},{8,12},{12,14},{14,10},{10,6},{6,2},{2,0},{1,5},{5,9},... | collective-permute-start | bytes 393224 | tf_op jit(solution)/shard_map/ppermute | solution.py:277
  38.5 0.7 collective-permute-start.9
  39.2 3.2 %collective-permute-done.8.refs_1_ = bf16[256,256]{1,0:T(8,128)(2,1)S(1)} collective-permute-done((bf16[256,256]{1,0:T(8,128)(2,1)}, bf16[256,256]{1,0:T(8,128)(2,1)S(1)}, u32[]{:S(2)}, u32[]{:S(2)}) %collective-permute-start.8) | collective-permute-done | bytes 131104 | tf_op jit(solution)/shard_map/ppermute | solution.py:277
  42.4 1.7 %collective-permute-start.10 = (bf16[256,256]{1,0:T(8,128)(2,1)S(1)}, bf16[256,256]{1,0:T(8,128)(2,1)S(1)}, u32[]{:S(2)}, u32[]{:S(2)}) collective-permute-start(bf16[256,256]{1,0:T(8,128)(2,1)S(1)} %collective-permute-done.8.refs_1_), channel_id=1, source_target_pairs={{0,4},{4,8},{8,12},{12,14},{14,10},{10,6},{6,2},{2,0},{1,5},{5,9},... | collective-permute-start | bytes 393224 | tf_op jit(solution)/shard_map/ppermute | solution.py:277
  44.7 2.7 %collective-permute-done.10.refs_3_ = bf16[256,256]{1,0:T(8,128)(2,1)S(1)} collective-permute-done((bf16[256,256]{1,0:T(8,128)(2,1)S(1)}, bf16[256,256]{1,0:T(8,128)(2,1)S(1)}, u32[]{:S(2)}, u32[]{:S(2)}) %collective-permute-start.10) | collective-permute-done | bytes 131104 | tf_op jit(solution)/shard_map/ppermute | solution.py:277
  47.4 1.7 %collective-permute-start.12 = (bf16[256,256]{1,0:T(8,128)(2,1)S(1)}, bf16[256,256]{1,0:T(8,128)(2,1)S(1)}, u32[]{:S(2)}, u32[]{:S(2)}) collective-permute-start(bf16[256,256]{1,0:T(8,128)(2,1)S(1)} %collective-permute-done.10.refs_3_), channel_id=1, source_target_pairs={{0,4},{4,8},{8,12},{12,14},{14,10},{10,6},{6,2},{2,0},{1,5},{5,9},... | collective-permute-start | bytes 393224 | tf_op jit(solution)/shard_map/ppermute | solution.py:277
  49.7 2.7 %collective-permute-done.12.refs_5_ = bf16[256,256]{1,0:T(8,128)(2,1)S(1)} collective-permute-done((bf16[256,256]{1,0:T(8,128)(2,1)S(1)}, bf16[256,256]{1,0:T(8,128)(2,1)S(1)}, u32[]{:S(2)}, u32[]{:S(2)}) %collective-permute-start.12) | collective-permute-done | bytes 131104 | tf_op jit(solution)/shard_map/ppermute | solution.py:277
  52.4 2.0 %collective-permute-start.14 = (bf16[256,256]{1,0:T(8,128)(2,1)S(1)}, bf16[256,256]{1,0:T(8,128)(2,1)S(1)}, u32[]{:S(2)}, u32[]{:S(2)}) collective-permute-start(bf16[256,256]{1,0:T(8,128)(2,1)S(1)} %collective-permute-done.12.refs_5_), channel_id=1, source_target_pairs={{0,4},{4,8},{8,12},{12,14},{14,10},{10,6},{6,2},{2,0},{1,5},{5,9},... | collective-permute-start | bytes 393224 | tf_op jit(solution)/shard_map/ppermute | solution.py:277
  54.4 3.0 %query.1.q_ref = bf16[256,512]{1,0:T(8,128)(2,1)} custom-call(s32[4]{0:T(128)} %pad_add_fusion.place, bf16[128,1536]{1,0:T(8,128)(2,1)} %get-tuple-element.8.own_ref, bf16[128,1536]{1,0:T(8,128)(2,1)} %copy-done.1, bf16[1536,512]{1,0:T(8,128)(2,1)} %weight.1), custom_call_target="tpu_custom_call" | custom-call | tf_op jit(solution)/shard_map/query/pallas_call | solution.py:261
  58.6 5.4 %attend.1.ctx_own = bf16[256,512]{1,0:T(8,128)(2,1)} custom-call(bf16[256,512]{1,0:T(8,128)(2,1)} %query.1.q_ref, bf16[256,256]{1,0:T(8,128)(2,1)} %keyvalue.1.refs_0_, bf16[256,256]{1,0:T(8,128)(2,1)} %copy-done.13, bf16[256,256]{1,0:T(8,128)(2,1)} %copy-done.14, bf16[256,256]{1,0:T(8,128)(2,1)} %copy-done.15, bf16[256,256]{1,0:T(8,128)(2,1)} %copy-done.16, ...), custom_call_target="tpu_custom_call" | custom-call | tf_op jit(solution)/shard_map/attend/pallas_call | solution.py:284
  64.6 1.4 %collective-permute-done.15.ctx_peer = bf16[256,512]{1,0:T(8,128)(2,1)S(1)} collective-permute-done((bf16[256,512]{1,0:T(8,128)(2,1)}, bf16[256,512]{1,0:T(8,128)(2,1)S(1)}, u32[]{:S(2)}, u32[]{:S(2)}) %collective-permute-start.15) | collective-permute-done | bytes 262176 | tf_op jit(solution)/shard_map/ppermute | solution.py:22
  66.0 0.7 %copy-done.11 = bf16[256,512]{1,0:T(8,128)(2,1)} copy-done((bf16[256,512]{1,0:T(8,128)(2,1)}, bf16[256,512]{1,0:T(8,128)(2,1)S(1)}, u32[]{:S(2)}) %copy-start.11) | copy-done | bytes 262168
  66.7 3.3 %finish.1 = bf16[256,768]{1,0:T(8,128)(2,1)} custom-call(s32[4]{0:T(128)} %pad_add_fusion.place, bf16[256,512]{1,0:T(8,128)(2,1)} %attend.1.ctx_own, bf16[256,512]{1,0:T(8,128)(2,1)} %copy-done.11, bf16[512,1536]{1,0:T(8,128)(2,1)} %w_own.1, bf16[512,768]{1,0:T(8,128)(2,1)} %copy-done.2, f32[128,768]{1,0:T(8,128)} %get-tuple-element.9.hid_own, ...), custom_call_target="tpu_custom_call" | custom-call | tf_op jit(solution)/shard_map/finish/pallas_call | solution.py:293
  (71 shorter events, 7.6 us)
Async XLA Ops:
  0.0 20.0 %collective-permute-start.6 = (bf16[2,768,1536]{2,1,0:T(8,128)(2,1)}, bf16[2,768,1536]{2,1,0:T(8,128)(2,1)}, u32[]{:S(2)}, u32[]{:S(2)}) collective-permute-start(bf16[2,768,1536]{2,1,0:T(8,128)(2,1)} %mix_own.1), channel_id=1, source_target_pairs={{0,1},{1,0},{2,3},{3,2},{4,5},{5,4},{6,7},{7,6},{8,9},{9,8},{10,11... | collective-permute-start | bytes 14155784 | tf_op jit(solution)/shard_map/ppermute | solution.py:22
  1.5 15.8 %collective-permute-start.1 = (bf16[192,768]{1,0:T(8,128)(2,1)S(1)}, bf16[192,768]{1,0:T(8,128)(2,1)S(1)}, u32[]{:S(2)}, u32[]{:S(2)}) collective-permute-start(bf16[192,768]{1,0:T(8,128)(2,1)S(1)} %get-tuple-element.12), channel_id=1, source_target_pairs={{0,2},{2,0},{4,6},{6,4},{8,10},{10,8},{12,14},{14,12},{1,3},{3,1},... | collective-permute-start | bytes 884744 | tf_op jit(solution)/shard_map/ppermute | solution.py:214
  4.1 13.3 %collective-permute-start.3 = (bf16[192,768]{1,0:T(8,128)(2,1)S(1)}, bf16[192,768]{1,0:T(8,128)(2,1)S(1)}, u32[]{:S(2)}, u32[]{:S(2)}) collective-permute-start(bf16[192,768]{1,0:T(8,128)(2,1)S(1)} %get-tuple-element.11), channel_id=1, source_target_pairs={{0,0},{14,14},{2,4},{4,2},{6,8},{8,6},{10,12},{12,10},{1,1},{15,15... | collective-permute-start | bytes 884744 | tf_op jit(solution)/shard_map/ppermute | solution.py:215
  4.8 15.1 %collective-permute-start = (bf16[256,768]{1,0:T(8,128)(2,1)}, bf16[256,768]{1,0:T(8,128)(2,1)S(1)}, u32[]{:S(2)}, u32[]{:S(2)}) collective-permute-start(bf16[256,768]{1,0:T(8,128)(2,1)} %x_own.1), channel_id=1, source_target_pairs={{0,1},{1,0},{2,3},{3,2},{4,5},{5,4},{6,7},{7,6},{8,9},{9,8},{10,11... | collective-permute-start | bytes 1179656 | tf_op jit(solution)/shard_map/ppermute | solution.py:22
  17.4 2.6 %collective-permute-start.2 = (bf16[192,768]{1,0:T(8,128)(2,1)S(1)}, bf16[192,768]{1,0:T(8,128)(2,1)S(1)}, u32[]{:S(2)}, u32[]{:S(2)}) collective-permute-start(bf16[192,768]{1,0:T(8,128)(2,1)S(1)} %collective-permute-done.1.near_own), channel_id=1, source_target_pairs={{0,1},{1,0},{2,3},{3,2},{4,5},{5,4},{6,7},{7,6},{8,9},{9,8},{10,11... | collective-permute-start | bytes 884744 | tf_op jit(solution)/shard_map/ppermute | solution.py:22
  17.4 2.6 %collective-permute-start.4 = (bf16[192,768]{1,0:T(8,128)(2,1)S(1)}, bf16[192,768]{1,0:T(8,128)(2,1)S(1)}, u32[]{:S(2)}, u32[]{:S(2)}) collective-permute-start(bf16[192,768]{1,0:T(8,128)(2,1)S(1)} %collective-permute-done.3.far_own), channel_id=1, source_target_pairs={{0,1},{1,0},{2,3},{3,2},{4,5},{5,4},{6,7},{7,6},{8,9},{9,8},{10,11... | collective-permute-start | bytes 884744 | tf_op jit(solution)/shard_map/ppermute | solution.py:22
  18.7 1.3 %collective-permute-start.5 = (f32[16,768]{1,0:T(8,128)S(1)}, f32[16,768]{1,0:T(8,128)S(1)}, u32[]{:S(2)}, u32[]{:S(2)}) collective-permute-start(f32[16,768]{1,0:T(8,128)S(1)} %maximum_maximum_fusion.small_own), channel_id=1, source_target_pairs={{0,1},{1,0},{2,3},{3,2},{4,5},{5,4},{6,7},{7,6},{8,9},{9,8},{10,11... | collective-permute-start | bytes 147464 | tf_op jit(solution)/shard_map/ppermute | solution.py:22
  19.5 11.3 %copy-start.3 = (bf16[1536,2,128]{2,1,0:T(2,128)(2,1)S(1)}, bf16[1536,2,128]{2,1,0:T(2,128)(2,1)}, u32[]{:S(2)}) copy-start(bf16[1536,2,128]{2,1,0:T(2,128)(2,1)} %param.14) | copy-start | bytes 2359300
  30.6 2.0 %collective-permute-start.7 = (bf16[128,1536]{1,0:T(8,128)(2,1)}, bf16[128,1536]{1,0:T(8,128)(2,1)S(1)}, u32[]{:S(2)}, u32[]{:S(2)}) collective-permute-start(bf16[128,1536]{1,0:T(8,128)(2,1)} %get-tuple-element.8.own_ref), channel_id=1, source_target_pairs={{0,1},{1,0},{2,3},{3,2},{4,5},{5,4},{6,7},{7,6},{8,9},{9,8},{10,11... | collective-permute-start | bytes 1179656 | tf_op jit(solution)/shard_map/ppermute | solution.py:22
  33.3 21.1 %copy-start.21 = (f32[128,768]{1,0:T(8,128)S(1)}, f32[128,768]{1,0:T(8,128)}, u32[]{:S(2)}) copy-start(f32[128,768]{1,0:T(8,128)} %get-tuple-element.10) | copy-start | bytes 1179652
  35.8 6.6 %collective-permute-start.8 = (bf16[256,256]{1,0:T(8,128)(2,1)}, bf16[256,256]{1,0:T(8,128)(2,1)S(1)}, u32[]{:S(2)}, u32[]{:S(2)}) collective-permute-start(bf16[256,256]{1,0:T(8,128)(2,1)} %keyvalue.1.refs_0_), channel_id=1, source_target_pairs={{0,4},{4,8},{8,12},{12,14},{14,10},{10,6},{6,2},{2,0},{1,5},{5,9},... | collective-permute-start | bytes 393224 | tf_op jit(solution)/shard_map/ppermute | solution.py:277
  38.4 26.2 %collective-permute-start.16 = (bf16[512,768]{1,0:T(8,128)(2,1)S(1)}, bf16[512,768]{1,0:T(8,128)(2,1)S(1)}, u32[]{:S(2)}, u32[]{:S(2)}) collective-permute-start(bf16[512,768]{1,0:T(8,128)(2,1)S(1)} %constant_dynamic-slice_fusion), channel_id=1, source_target_pairs={{0,1},{1,0},{2,3},{3,2},{4,5},{5,4},{6,7},{7,6},{8,9},{9,8},{10,11... | collective-permute-start | bytes 2359304 | tf_op jit(solution)/shard_map/ppermute | solution.py:22
  38.5 5.9 %collective-permute-start.9 = (bf16[256,256]{1,0:T(8,128)(2,1)S(1)}, bf16[256,256]{1,0:T(8,128)(2,1)S(1)}, u32[]{:S(2)}, u32[]{:S(2)}) collective-permute-start(bf16[256,256]{1,0:T(8,128)(2,1)S(1)} %copy-done.4), channel_id=1, source_target_pairs={{4,0},{8,4},{12,8},{14,12},{10,14},{6,10},{2,6},{0,2},{5,1},{9,5},... | collective-permute-start | bytes 393224 | tf_op jit(solution)/shard_map/ppermute | solution.py:280
  42.4 15.0 %copy-start.13 = (bf16[256,256]{1,0:T(8,128)(2,1)}, bf16[256,256]{1,0:T(8,128)(2,1)S(1)}, u32[]{:S(2)}) copy-start(bf16[256,256]{1,0:T(8,128)(2,1)S(1)} %collective-permute-done.8.refs_1_) | copy-start | bytes 393220
  42.4 5.1 %collective-permute-start.10 = (bf16[256,256]{1,0:T(8,128)(2,1)S(1)}, bf16[256,256]{1,0:T(8,128)(2,1)S(1)}, u32[]{:S(2)}, u32[]{:S(2)}) collective-permute-start(bf16[256,256]{1,0:T(8,128)(2,1)S(1)} %collective-permute-done.8.refs_1_), channel_id=1, source_target_pairs={{0,4},{4,8},{8,12},{12,14},{14,10},{10,6},{6,2},{2,0},{1,5},{5,9},... | collective-permute-start | bytes 393224 | tf_op jit(solution)/shard_map/ppermute | solution.py:277
  44.4 13.0 %copy-start.14 = (bf16[256,256]{1,0:T(8,128)(2,1)}, bf16[256,256]{1,0:T(8,128)(2,1)S(1)}, u32[]{:S(2)}) copy-start(bf16[256,256]{1,0:T(8,128)(2,1)S(1)} %collective-permute-done.9.refs_2_) | copy-start | bytes 393220
  44.4 5.0 %collective-permute-start.11 = (bf16[256,256]{1,0:T(8,128)(2,1)S(1)}, bf16[256,256]{1,0:T(8,128)(2,1)S(1)}, u32[]{:S(2)}, u32[]{:S(2)}) collective-permute-start(bf16[256,256]{1,0:T(8,128)(2,1)S(1)} %collective-permute-done.9.refs_2_), channel_id=1, source_target_pairs={{4,0},{8,4},{12,8},{14,12},{10,14},{6,10},{2,6},{0,2},{5,1},{9,5},... | collective-permute-start | bytes 393224 | tf_op jit(solution)/shard_map/ppermute | solution.py:280
  47.4 10.0 %copy-start.15 = (bf16[256,256]{1,0:T(8,128)(2,1)}, bf16[256,256]{1,0:T(8,128)(2,1)S(1)}, u32[]{:S(2)}) copy-start(bf16[256,256]{1,0:T(8,128)(2,1)S(1)} %collective-permute-done.10.refs_3_) | copy-start | bytes 393220
  47.4 5.0 %collective-permute-start.12 = (bf16[256,256]{1,0:T(8,128)(2,1)S(1)}, bf16[256,256]{1,0:T(8,128)(2,1)S(1)}, u32[]{:S(2)}, u32[]{:S(2)}) collective-permute-start(bf16[256,256]{1,0:T(8,128)(2,1)S(1)} %collective-permute-done.10.refs_3_), channel_id=1, source_target_pairs={{0,4},{4,8},{8,12},{12,14},{14,10},{10,6},{6,2},{2,0},{1,5},{5,9},... | collective-permute-start | bytes 393224 | tf_op jit(solution)/shard_map/ppermute | solution.py:277
  49.4 8.0 %copy-start.16 = (bf16[256,256]{1,0:T(8,128)(2,1)}, bf16[256,256]{1,0:T(8,128)(2,1)S(1)}, u32[]{:S(2)}) copy-start(bf16[256,256]{1,0:T(8,128)(2,1)S(1)} %collective-permute-done.11.refs_4_) | copy-start | bytes 393220
  49.4 7.9 %collective-permute-start.13 = (bf16[256,256]{1,0:T(8,128)(2,1)S(1)}, bf16[256,256]{1,0:T(8,128)(2,1)S(1)}, u32[]{:S(2)}, u32[]{:S(2)}) collective-permute-start(bf16[256,256]{1,0:T(8,128)(2,1)S(1)} %collective-permute-done.11.refs_4_), channel_id=1, source_target_pairs={{4,0},{8,4},{12,8},{14,12},{10,14},{6,10},{2,6},{0,2},{5,1},{9,5},... | collective-permute-start | bytes 393224 | tf_op jit(solution)/shard_map/ppermute | solution.py:280
  52.4 5.0 %collective-permute-start.14 = (bf16[256,256]{1,0:T(8,128)(2,1)S(1)}, bf16[256,256]{1,0:T(8,128)(2,1)S(1)}, u32[]{:S(2)}, u32[]{:S(2)}) collective-permute-start(bf16[256,256]{1,0:T(8,128)(2,1)S(1)} %collective-permute-done.12.refs_5_), channel_id=1, source_target_pairs={{0,4},{4,8},{8,12},{12,14},{14,10},{10,6},{6,2},{2,0},{1,5},{5,9},... | collective-permute-start | bytes 393224 | tf_op jit(solution)/shard_map/ppermute | solution.py:277
  54.4 10.2 %collective-permute-start.17 = (f32[128,768]{1,0:T(8,128)S(1)}, f32[128,768]{1,0:T(8,128)S(1)}, u32[]{:S(2)}, u32[]{:S(2)}) collective-permute-start(f32[128,768]{1,0:T(8,128)S(1)} %copy-done.21), channel_id=1, source_target_pairs={{0,1},{1,0},{2,3},{3,2},{4,5},{5,4},{6,7},{7,6},{8,9},{9,8},{10,11... | collective-permute-start | bytes 1179656 | tf_op jit(solution)/shard_map/ppermute | solution.py:22
  64.1 1.9 %collective-permute-start.15 = (bf16[256,512]{1,0:T(8,128)(2,1)}, bf16[256,512]{1,0:T(8,128)(2,1)S(1)}, u32[]{:S(2)}, u32[]{:S(2)}) collective-permute-start(bf16[256,512]{1,0:T(8,128)(2,1)} %attend.1.ctx_own), channel_id=1, source_target_pairs={{0,1},{1,0},{2,3},{3,2},{4,5},{5,4},{6,7},{7,6},{8,9},{9,8},{10,11... | collective-permute-start | bytes 786440 | tf_op jit(solution)/shard_map/ppermute | solution.py:22
  (16 other events, 30.4 us)

commit v2 on v1

--- a/solution.py
+++ b/solution.py
@@ -156,40 +156,76 @@
     out[pl.ds(back, count), :] = jnp.dot(peer_ref[...], weight[...], preferred_element_type=F32).astype(BF16)
 
 
-def attend_kernel(q_ref, *refs, scale):
-    blocks, out = refs[:-1], refs[-1]
+def attend_kernel(*refs, count, scale, first, last):
+    q_ref, blocks, refs = refs[0], refs[1 : 1 + count], refs[1 + count :]
+    state_in, refs = ((), refs) if first else (refs[:2], refs[2:])
     factor = scale * math.log2(math.e)
     heads = q_ref.shape[1] // HD
     for head in range(heads):
-        q = q_ref[:, head * HD : (head + 1) * HD]
+        cols = slice(head * HD, (head + 1) * HD)
+        q = q_ref[:, cols]
         scores = [
             lax.dot_general(q, kv[:, 0:HD], (((1,), (1,)), ((), ())), preferred_element_type=F32) for kv in blocks
         ]
-        peak = functools.reduce(jnp.maximum, [jnp.max(s, axis=1, keepdims=True) for s in scores])
+        peaks = [jnp.max(s, axis=1, keepdims=True) for s in scores]
         total = None
         context = None
+        if not first:
+            stats, summed = state_in
+            before = stats[:, head : head + 1]
+            peaks.append(before)
+        peak = functools.reduce(jnp.maximum, peaks)
+        if not first:
+            keep = jnp.exp2((before - peak) * factor)
+            total = stats[:, heads + head : heads + head + 1] * keep
+            context = summed[:, cols] * keep
         for s, kv in zip(scores, blocks):
             probs = jnp.exp2((s - peak) * factor)
             part = jnp.sum(probs, axis=1, keepdims=True)
             value = jnp.dot(probs.astype(BF16), kv[:, HD:], preferred_element_type=F32)
             total = part if total is None else total + part
             context = value if context is None else context + value
-        out[:, head * HD : (head + 1) * HD] = (context / total).astype(BF16)
-
-
-def finish_kernel(place, ctx_own, ctx_peer, w_own, w_peer, hid_own, hid_peer, out):
-    count = hid_own.shape[0]
-    width = hid_own.shape[1]
+        if last:
+            refs[0][:, cols] = (context / total).astype(BF16)
+        else:
+            refs[0][:, head : head + 1] = peak
+            refs[0][:, heads + head : heads + head + 1] = total
+            refs[1][:, cols] = context
+
+
+def begin_kernel(place, ctx, w_own, hid_own, hid_peer, out):
+    count, width = hid_own.shape
     cols = pl.ds(pl.multiple_of(place[0] * width, 128), width)
     for at, hid in ((place[0] * count, hid_own), ((1 - place[0]) * count, hid_peer)):
         rows = pl.ds(pl.multiple_of(at, count), count)
-        mixed = jnp.dot(ctx_own[rows, :], w_own[:, cols], preferred_element_type=F32)
-        mixed = mixed + jnp.dot(ctx_peer[rows, :], w_peer[...], preferred_element_type=F32)
-        out[rows, :] = (hid[...] + mixed).astype(BF16)
-
-
-def params(limit=100 << 20):
-    return pltpu.CompilerParams(vmem_limit_bytes=56 << 20)
+        out[rows, :] = hid[...] + jnp.dot(ctx[rows, :], w_own[:, cols], preferred_element_type=F32)
+
+
+def finish_kernel(place, ctx, w_peer, partial, out):
+    width = partial.shape[1]
+    cols = pl.ds(pl.multiple_of(place[0] * width, 128), width)
+    mixed = jnp.dot(ctx[...], w_peer[:, cols], preferred_element_type=F32)
+    out[...] = (partial[...] + mixed).astype(BF16)
+
+
+def call(kernel, outs, name, mebibytes, *operands, specs=None, scratch=(), hbm_out=False):
+    held, in_specs = [], []
+    for i, operand in enumerate(operands):
+        spec = (specs or {}).get(i, VMEM)
+        in_specs.append(spec)
+        space = pltpu.VMEM if spec is VMEM else pltpu.HBM if spec is ANY else None
+        held.append(pltpu.with_memory_space_constraint(operand, space) if space else operand)
+    shapes = tuple((jax.ShapeDtypeStruct if hbm_out else pltpu.VMEM)(shape, dtype) for shape, dtype in outs)
+    result = pl.pallas_call(
+        kernel,
+        out_shape=shapes,
+        in_specs=in_specs,
+        out_specs=(VMEM,) * len(shapes),
+        scratch_shapes=list(scratch),
+        compiler_params=pltpu.CompilerParams(vmem_limit_bytes=mebibytes << 20),
+        name=name,
+    )(*held)
+    return result if len(outs) > 1 else result[0]
 
 
 def local(seq_in, conv_gain, dw_kernel, mix_weight, attn_gain, q_weight, kv_weight, out_weight):
@@ -211,37 +247,40 @@
     far_pairs = [(0, 0), (size - 1, size - 1)]
     for i in range(1, size - 1, 2):
         far_pairs += [(i, i + 1), (i + 1, i)]
-    near = lax.ppermute(jnp.where(even, high, low), "seq", near_pairs)
-    far = lax.ppermute(jnp.where(even, low, high), "seq", far_pairs)
+    to_near, to_far, x_sent, mix_sent, out_sent = lax.optimization_barrier(
+        (jnp.where(even, high, low), jnp.where(even, low, high), seq_in, mix_weight, out_weight)
+    )
+    near = lax.ppermute(to_near, "seq", near_pairs)
+    far = lax.ppermute(to_far, "seq", far_pairs)
 
     small = jnp.concatenate(
         [conv_gain, dw_kernel.reshape(2 * taps, width), attn_gain[None, :], jnp.zeros((3, width), F32)], axis=0
     )
     small_peer = peer(small)
-    x_peer = peer(seq_in)
-    mix_peer = peer(mix_weight)
-    out_away = lax.dynamic_slice_in_dim(out_weight, (1 - core) * width, width, axis=1)
-    out_peer = peer(out_away)
-    near_peer = peer(near)
-    far_peer = peer(far)
-
+    x_peer = peer(x_sent)
+    mix_peer = peer(mix_sent)
+    out_peer = peer(out_sent)
     bottom = rows + reach
     place = jnp.stack(
         [core, me * rows, jnp.where(even, bottom, 0), jnp.where(even, 0, bottom)]
     ).astype(jnp.int32)
-
-    features, hidden_own, hidden_away = pl.pallas_call(
+    kv_flat = kv_weight.reshape(2 * width, 2 * kv_weight.shape[2])
+    near, far, small, small_peer, x_peer, place, kv_flat = lax.optimization_barrier(
+        (near, far, small, small_peer, x_peer, place, kv_flat)
+    )
+    near_peer = peer(near)
+    far_peer = peer(far)
+
+    features, hidden_own, hidden_away = call(
         functools.partial(
             tower_kernel, rows=rows, first=first, second=second, length=rows * size, taps=taps
         ),
-        out_shape=(
-            jax.ShapeDtypeStruct((mine, 2 * width), BF16),
-            jax.ShapeDtypeStruct((mine, width), F32),
-            jax.ShapeDtypeStruct((mine, width), F32),
-        ),
-        in_specs=[SMEM] + [VMEM] * 8 + [ANY] * 2,
-        out_specs=(VMEM, VMEM, VMEM),
-        scratch_shapes=[
+        [((mine, 2 * width), BF16), ((mine, width), F32), ((mine, width), F32)],
+        "tower",
+        24,
+        place, seq_in, x_peer, near, near_peer, far, far_peer, small, small_peer, mix_weight, mix_peer,
+        specs={0: SMEM, 9: ANY, 10: ANY},
+        scratch=[
             pltpu.VMEM((2, rows + 2 * reach, width), BF16),
             pltpu.VMEM((2, span, width), F32),
             pltpu.VMEM((2, lead, width), F32),
@@ -250,54 +289,60 @@
             pltpu.VMEM((2, 2, width, 2 * width), BF16),
             pltpu.SemaphoreType.DMA((2, 2)),
         ],
-        compiler_params=params(),
-        name="tower",
-    )(place, seq_in, x_peer, near, near_peer, far, far_peer, small, small_peer, mix_weight, mix_peer)
+    )
 
     features_peer = peer(features)
-    kv_width = 2 * kv_weight.shape[2]
 
     def project(weight, name):
-        return pl.pallas_call(
-            project_kernel,
-            out_shape=jax.ShapeDtypeStruct((rows, weight.shape[1]), BF16),
-            in_specs=[SMEM, VMEM, VMEM, VMEM],
-            out_specs=VMEM,
-            compiler_params=params(),
-            name=name,
-        )(place, features, features_peer, weight)
-
-    kv = project(kv_weight.reshape(2 * width, kv_width), "keyvalue")
+        return call(
+            project_kernel, [((rows, weight.shape[1]), BF16)], name, 4, place, features, features_peer, weight,
+            specs={0: SMEM},
+        )
+
+    kv = project(kv_flat, "keyvalue")
     order = ring_order(size)
     ahead = [(order[i], order[(i + 1) % size]) for i in range(size)]
     behind = [(b, a) for a, b in ahead]
-    blocks = [kv]
+    queries = None
+    heads = q_weight.shape[1] // HD
+    state = ()
+    fresh = [kv]
     up = down = kv
     for step in range(size // 2):
         up = lax.ppermute(up, "seq", ahead)
-        blocks.append(up)
+        arrived = [up]
         if 2 * step + 2 < size:
             down = lax.ppermute(down, "seq", behind)
-            blocks.append(down)
-    hidden_peer = peer(hidden_away)
-    queries = project(q_weight, "query")
-    context = pl.pallas_call(
-        functools.partial(attend_kernel, scale=1.0 / math.sqrt(HD)),
-        out_shape=jax.ShapeDtypeStruct(queries.shape, BF16),
-        in_specs=[VMEM] * (1 + len(blocks)),
-        out_specs=VMEM,
-        compiler_params=params(),
-        name="attend",
-    )(queries, *blocks)
+            arrived.append(down)
+        if queries is None:
+            queries = project(q_weight, "query")
+            hidden_peer = peer(hidden_away)
+        state = call(
+            functools.partial(attend_kernel, count=len(fresh), scale=1.0 / math.sqrt(HD), first=step == 0, last=False),
+            [((rows, HD), F32), ((rows, heads * HD), F32)],
+            "attend%d" % step,
+            8,
+            queries, *fresh, *state,
+        )
+        if step + 1 < size // 2:
+            up, down, *state = lax.optimization_barrier((up, down, *state))
+            arrived = [up, down]
+        fresh = arrived
+    context = call(
+        functools.partial(attend_kernel, count=len(fresh), scale=1.0 / math.sqrt(HD), first=False, last=True),
+        [((rows, heads * HD), BF16)],
+        "attend_last",
+        8,
+        queries, *fresh, *state,
+    )
     context_peer = peer(context)
-    return pl.pallas_call(
-        finish_kernel,
-        out_shape=jax.ShapeDtypeStruct((rows, width), BF16),
-        in_specs=[SMEM] + [VMEM] * 6,
-        out_specs=VMEM,
-        compiler_params=params(),
-        name="finish",
-    )(place, context, context_peer, out_weight, out_peer, hidden_own, hidden_peer)
+    partial = call(
+        begin_kernel, [((rows, width), F32)], "begin", 8, place, context, out_weight, hidden_own, hidden_peer, specs={0: SMEM}
+    )
+    return call(
+        finish_kernel, [((rows, width), BF16)], "finish", 8, place, context_peer, out_peer, partial,
+        specs={0: SMEM}, hbm_out=True,
+    )
 
 
 def solution(mesh):

time: 70.4 us -> 63 us (0.89)
  local copies, waits for them, and re-layouts: 6.22 us -> 2.79 us
  Pallas kernels: 23.8 us -> 21.1 us
  starting transfers between devices: 14.7 us -> 12.2 us
  waiting for transfers between devices: 22.6 us -> 23.7 us
    ppermute x3, waiting for transfers between devices: 0.63 us -> 4.68 us  [local(): down = lax.ppermute(down, 'seq', behind)]
    unnamed x46 -> x8, local copies, waits for them, and re-layouts: 5.39 us -> 2.01 us
    ppermute x2, waiting for transfers between devices: 10.8 us -> 7.48 us  [the longest x1 7.47 us: local(): near = lax.ppermute(to_near, 'seq', near_pairs)]
    pallas_call x5 -> x10, Pallas kernels: 23.8 us -> 21.1 us  [call(): pl.pallas_call(kernel, out_shape=shapes, in_specs=in_specs, out_specs=(VM...]
    ppermute x4, starting transfers between devices: 7.93 us -> 5.99 us  [local(): up = lax.ppermute(up, 'seq', ahead)]
    ppermute x9, waiting for transfers between devices: 2.62 us -> 4.54 us  [peer(): return lax.ppermute(array, 'ch', SWAP)]
    ppermute x4, waiting for transfers between devices: 8.57 us -> 7 us  [local(): up = lax.ppermute(up, 'seq', ahead)]
    select_n x1, other arithmetic: 1.09 us -> 1.95 us  [local(): jnp.where(even, low, high)]
  transfers between devices with their start and end apart: 18 -> 18, of which waited for: 9 -> 13; matrix products, arithmetic and copies ran while one was open for 7% -> 6% of each run, Pallas kernels for 12% -> 31%
where the time goes in v2:
time: 63 us; the launch traced here: 62.7 us
  waiting for transfers between devices  23.7 us (38%)
  Pallas kernels  21.1 us (33%)
  starting transfers between devices  12.2 us (19%)
  local copies, waits for them, and re-layouts  2.79 us (4%)
  other arithmetic  2.79 us (4%)
    pallas_call x10, Pallas kernels, call(): pl.pallas_call(kernel, out_shape=shapes, in_specs=in_specs, out_specs=(VM...  21.1 us
    ppermute x1, waiting for transfers between devices, local(): near = lax.ppermute(to_near, 'seq', near_pairs)  7.47 us
    ppermute x4, waiting for transfers between devices, local(): up = lax.ppermute(up, 'seq', ahead)  7 us
    ppermute x4, starting transfers between devices, local(): up = lax.ppermute(up, 'seq', ahead)  5.99 us
    ppermute x3, waiting for transfers between devices, local(): down = lax.ppermute(down, 'seq', behind)  4.68 us
    ppermute x9, waiting for transfers between devices, peer(): return lax.ppermute(array, 'ch', SWAP)  4.54 us
    ppermute x1, starting transfers between devices, local(): near = lax.ppermute(to_near, 'seq', near_pairs)  2.97 us
    unnamed x8, local copies, waits for them, and re-layouts  2.01 us
  transfers between devices with their start and end apart: 18, of which 13 were waited for; matrix products, arithmetic and copies ran while one was open for 6% of the time, Pallas kernels for 31%

profile of v2, /device:TPU:0, one launch (start us, length us, event | category | flops | bytes accessed | tf_op | source)
XLA Modules:
  0.0 62.7 jit_solution(10721223609183655309)
XLA Ops:
  0.0 1.9 %broadcast_select_fusion = (bf16[192,768]{1,0:T(8,128)(2,1)S(1)}, bf16[192,768]{1,0:T(8,128)(2,1)}) fusion(pred[]{:T(512)S(6)} %eq.5, bf16[256,768]{1,0:T(8,128)(2,1)} %x_own.1), kind=kLoop, calls=%fused_computation.1 | loop fusion | flops 294912 | bytes 1179649 | tf_op jit(solution)/shard_map/jit(_where)/select_n | solution.py:251
  2.5 3.0 %collective-permute-start = (bf16[192,768]{1,0:T(8,128)(2,1)}, bf16[192,768]{1,0:T(8,128)(2,1)S(1)}, u32[]{:S(2)}, u32[]{:S(2)}) collective-permute-start(bf16[192,768]{1,0:T(8,128)(2,1)} %get-tuple-element.40), channel_id=1, source_target_pairs={{0,2},{2,0},{4,6},{6,4},{8,10},{10,8},{12,14},{14,12},{1,3},{3,1},... | collective-permute-start | bytes 884744 | tf_op jit(solution)/shard_map/ppermute | solution.py:253
  8.4 1.2 %copy.13 = bf16[192,8,2,128]{3,1,2,0:T(8,128)(2,1)S(1)} copy(bf16[192,8,2,128]{3,2,1,0:T(2,128)(2,1)} %bitcast.9) | data formatting | bytes 1572864
  11.0 7.5 %collective-permute-done.near_own = bf16[192,768]{1,0:T(8,128)(2,1)S(1)} collective-permute-done((bf16[192,768]{1,0:T(8,128)(2,1)}, bf16[192,768]{1,0:T(8,128)(2,1)S(1)}, u32[]{:S(2)}, u32[]{:S(2)}) %collective-permute-start) | collective-permute-done | bytes 294944 | tf_op jit(solution)/shard_map/ppermute | solution.py:253
  19.0 1.1 %collective-permute-done.4.near_peer = bf16[192,768]{1,0:T(8,128)(2,1)S(1)} collective-permute-done((bf16[192,768]{1,0:T(8,128)(2,1)S(1)}, bf16[192,768]{1,0:T(8,128)(2,1)S(1)}, u32[]{:S(2)}, u32[]{:S(2)}) %collective-permute-start.4) | collective-permute-done | bytes 294944 | tf_op jit(solution)/shard_map/ppermute | solution.py:22
  20.5 7.8 %tower.1 = (bf16[128,1536]{1,0:T(8,128)(2,1)S(1)}, f32[128,768]{1,0:T(8,128)S(1)}, f32[128,768]{1,0:T(8,128)S(1)}) custom-call(s32[4]{0:T(128)S(1)} %pad_add_fusion.place, bf16[256,768]{1,0:T(8,128)(2,1)S(1)} %copy-done, bf16[256,768]{1,0:T(8,128)(2,1)S(1)} %collective-permute-done.3.x_peer, bf16[192,768]{1,0:T(8,128)(2,1)S(1)} %collective-permute-done.near_own, ...), custom_call_target="tpu_custom_call" | custom-call | tf_op jit(solution)/shard_map/tower/pallas_call | solution.py:219
  28.5 1.6 %collective-permute-done.7.peer_ref = bf16[128,1536]{1,0:T(8,128)(2,1)S(1)} collective-permute-done((bf16[128,1536]{1,0:T(8,128)(2,1)S(1)}, bf16[128,1536]{1,0:T(8,128)(2,1)S(1)}, u32[]{:S(2)}, u32[]{:S(2)}) %collective-permute-start.7) | collective-permute-done | bytes 393248 | tf_op jit(solution)/shard_map/ppermute | solution.py:22
  31.0 2.5 %collective-permute-start.8 = (bf16[256,256]{1,0:T(8,128)(2,1)S(1)}, bf16[256,256]{1,0:T(8,128)(2,1)S(1)}, u32[]{:S(2)}, u32[]{:S(2)}) collective-permute-start(bf16[256,256]{1,0:T(8,128)(2,1)S(1)} %keyvalue.1.refs_1_), channel_id=1, source_target_pairs={{0,4},{4,8},{8,12},{12,14},{14,10},{10,6},{6,2},{2,0},{1,5},{5,9},... | collective-permute-start | bytes 393224 | tf_op jit(solution)/shard_map/ppermute | solution.py:312
  33.5 1.1 %query.1.refs_0_ = bf16[256,512]{1,0:T(8,128)(2,1)S(1)} custom-call(s32[4]{0:T(128)S(1)} %pad_add_fusion.place, bf16[128,1536]{1,0:T(8,128)(2,1)S(1)} %get-tuple-element.50.own_ref, bf16[128,1536]{1,0:T(8,128)(2,1)S(1)} %collective-permute-done.7.peer_ref, bf16[1536,512]{1,0:T(8,128)(2,1)S(1)} %copy-done.1), custom_call_target="tpu_custom_call" | custom-call | tf_op jit(solution)/shard_map/query/pallas_call | solution.py:219
  35.5 1.8 %collective-permute-done.8.refs_1_ = bf16[256,256]{1,0:T(8,128)(2,1)S(1)} collective-permute-done((bf16[256,256]{1,0:T(8,128)(2,1)S(1)}, bf16[256,256]{1,0:T(8,128)(2,1)S(1)}, u32[]{:S(2)}, u32[]{:S(2)}) %collective-permute-start.8) | collective-permute-done | bytes 131104 | tf_op jit(solution)/shard_map/ppermute | solution.py:312
  37.3 1.5 %collective-permute-done.9.refs_2_ = bf16[256,256]{1,0:T(8,128)(2,1)S(1)} collective-permute-done((bf16[256,256]{1,0:T(8,128)(2,1)S(1)}, bf16[256,256]{1,0:T(8,128)(2,1)S(1)}, u32[]{:S(2)}, u32[]{:S(2)}) %collective-permute-start.9) | collective-permute-done | bytes 131104 | tf_op jit(solution)/shard_map/ppermute | solution.py:315
  38.8 1.6 %collective-permute-start.10 = (bf16[256,256]{1,0:T(8,128)(2,1)S(1)}, bf16[256,256]{1,0:T(8,128)(2,1)S(1)}, u32[]{:S(2)}, u32[]{:S(2)}) collective-permute-start(bf16[256,256]{1,0:T(8,128)(2,1)S(1)} %collective-permute-done.8.refs_1_), channel_id=1, source_target_pairs={{0,4},{4,8},{8,12},{12,14},{14,10},{10,6},{6,2},{2,0},{1,5},{5,9},... | collective-permute-start | bytes 393224 | tf_op jit(solution)/shard_map/ppermute | solution.py:312
  40.8 1.7 %attend1.1 = (f32[256,128]{1,0:T(8,128)S(1)}, f32[256,512]{1,0:T(8,128)S(1)}) custom-call(bf16[256,512]{1,0:T(8,128)(2,1)S(1)} %query.1.refs_0_, bf16[256,256]{1,0:T(8,128)(2,1)S(1)} %collective-permute-done.8.refs_1_, bf16[256,256]{1,0:T(8,128)(2,1)S(1)} %collective-permute-done.9.refs_2_, f32[256,128]{1,0:T(8,128)S(1)} %get-tuple-element.56.refs_3_, ...), custom_call_target="tpu_custom_call" | custom-call | tf_op jit(solution)/shard_map/attend1/pallas_call | solution.py:219
  42.5 1.2 %collective-permute-done.10.refs_1_ = bf16[256,256]{1,0:T(8,128)(2,1)S(1)} collective-permute-done((bf16[256,256]{1,0:T(8,128)(2,1)S(1)}, bf16[256,256]{1,0:T(8,128)(2,1)S(1)}, u32[]{:S(2)}, u32[]{:S(2)}) %collective-permute-start.10) | collective-permute-done | bytes 131104 | tf_op jit(solution)/shard_map/ppermute | solution.py:312
  43.7 1.6 %collective-permute-done.11.refs_2_ = bf16[256,256]{1,0:T(8,128)(2,1)S(1)} collective-permute-done((bf16[256,256]{1,0:T(8,128)(2,1)S(1)}, bf16[256,256]{1,0:T(8,128)(2,1)S(1)}, u32[]{:S(2)}, u32[]{:S(2)}) %collective-permute-start.11) | collective-permute-done | bytes 131104 | tf_op jit(solution)/shard_map/ppermute | solution.py:315
  45.3 1.6 %collective-permute-start.12 = (bf16[256,256]{1,0:T(8,128)(2,1)S(1)}, bf16[256,256]{1,0:T(8,128)(2,1)S(1)}, u32[]{:S(2)}, u32[]{:S(2)}) collective-permute-start(bf16[256,256]{1,0:T(8,128)(2,1)S(1)} %collective-permute-done.10.refs_1_), channel_id=1, source_target_pairs={{0,4},{4,8},{8,12},{12,14},{14,10},{10,6},{6,2},{2,0},{1,5},{5,9},... | collective-permute-start | bytes 393224 | tf_op jit(solution)/shard_map/ppermute | solution.py:312
  47.3 1.8 %attend2.1 = (f32[256,128]{1,0:T(8,128)S(1)}, f32[256,512]{1,0:T(8,128)S(1)}) custom-call(bf16[256,512]{1,0:T(8,128)(2,1)S(1)} %query.1.refs_0_, bf16[256,256]{1,0:T(8,128)(2,1)S(1)} %collective-permute-done.10.refs_1_, bf16[256,256]{1,0:T(8,128)(2,1)S(1)} %collective-permute-done.11.refs_2_, f32[256,128]{1,0:T(8,128)S(1)} %get-tuple-element.62.refs_3_, ...), custom_call_target="tpu_custom_call" | custom-call | tf_op jit(solution)/shard_map/attend2/pallas_call | solution.py:219
  49.1 1.2 %collective-permute-done.12.refs_1_ = bf16[256,256]{1,0:T(8,128)(2,1)S(1)} collective-permute-done((bf16[256,256]{1,0:T(8,128)(2,1)S(1)}, bf16[256,256]{1,0:T(8,128)(2,1)S(1)}, u32[]{:S(2)}, u32[]{:S(2)}) %collective-permute-start.12) | collective-permute-done | bytes 131104 | tf_op jit(solution)/shard_map/ppermute | solution.py:312
  50.3 1.6 %collective-permute-done.13.refs_2_ = bf16[256,256]{1,0:T(8,128)(2,1)S(1)} collective-permute-done((bf16[256,256]{1,0:T(8,128)(2,1)S(1)}, bf16[256,256]{1,0:T(8,128)(2,1)S(1)}, u32[]{:S(2)}, u32[]{:S(2)}) %collective-permute-start.13) | collective-permute-done | bytes 131104 | tf_op jit(solution)/shard_map/ppermute | solution.py:315
  52.2 1.7 %attend3.1 = (f32[256,128]{1,0:T(8,128)S(1)}, f32[256,512]{1,0:T(8,128)S(1)}) custom-call(bf16[256,512]{1,0:T(8,128)(2,1)S(1)} %query.1.refs_0_, bf16[256,256]{1,0:T(8,128)(2,1)S(1)} %collective-permute-done.12.refs_1_, bf16[256,256]{1,0:T(8,128)(2,1)S(1)} %collective-permute-done.13.refs_2_, f32[256,128]{1,0:T(8,128)S(1)} %get-tuple-element.68.refs_3_, ...), custom_call_target="tpu_custom_call" | custom-call | tf_op jit(solution)/shard_map/attend3/pallas_call | solution.py:219
  54.0 2.9 %collective-permute-done.14.refs_1_ = bf16[256,256]{1,0:T(8,128)(2,1)S(1)} collective-permute-done((bf16[256,256]{1,0:T(8,128)(2,1)S(1)}, bf16[256,256]{1,0:T(8,128)(2,1)S(1)}, u32[]{:S(2)}, u32[]{:S(2)}) %collective-permute-start.14) | collective-permute-done | bytes 131104 | tf_op jit(solution)/shard_map/ppermute | solution.py:312
  56.8 2.6 %attend_last.1.ctx = bf16[256,512]{1,0:T(8,128)(2,1)S(1)} custom-call(bf16[256,512]{1,0:T(8,128)(2,1)S(1)} %query.1.refs_0_, bf16[256,256]{1,0:T(8,128)(2,1)S(1)} %collective-permute-done.14.refs_1_, f32[256,128]{1,0:T(8,128)S(1)} %get-tuple-element.70.refs_2_, f32[256,512]{1,0:T(8,128)S(1)} %get-tuple-element.71.refs_3_), custom_call_target="tpu_custom_call" | custom-call | tf_op jit(solution)/shard_map/attend_last/pallas_call | solution.py:219
  59.5 0.9 %begin.1.partial = f32[256,768]{1,0:T(8,128)S(1)} custom-call(s32[4]{0:T(128)S(1)} %pad_add_fusion.place, bf16[256,512]{1,0:T(8,128)(2,1)S(1)} %attend_last.1.ctx, bf16[512,1536]{1,0:T(8,128)(2,1)S(1)} %copy-done.2, f32[128,768]{1,0:T(8,128)S(1)} %get-tuple-element.73.hid_own, f32[128,768]{1,0:T(8,128)S(1)} %collective-permute-done.17.hid_peer), custom_call_target="tpu_custom_call" | custom-call | tf_op jit(solution)/shard_map/begin/pallas_call | solution.py:219
  61.0 1.7 %finish.1 = bf16[256,768]{1,0:T(8,128)(2,1)} custom-call(s32[4]{0:T(128)S(1)} %pad_add_fusion.place, bf16[256,512]{1,0:T(8,128)(2,1)S(1)} %collective-permute-done.15.ctx, bf16[512,1536]{1,0:T(8,128)(2,1)S(1)} %collective-permute-done.16.w_peer, f32[256,768]{1,0:T(8,128)S(1)} %begin.1.partial), custom_call_target="tpu_custom_call" | custom-call | tf_op jit(solution)/shard_map/finish/pallas_call | solution.py:219
  (37 shorter events, 9.6 us)
Async XLA Ops:
  0.0 20.5 %copy-start = (bf16[256,768]{1,0:T(8,128)(2,1)S(1)}, bf16[256,768]{1,0:T(8,128)(2,1)}, u32[]{:S(2)}) copy-start(bf16[256,768]{1,0:T(8,128)(2,1)} %x_own.1) | copy-start | bytes 1179652
  0.0 10.6 %copy-start.2 = (bf16[512,1536]{1,0:T(8,128)(2,1)S(1)}, bf16[512,1536]{1,0:T(8,128)(2,1)}, u32[]{:S(2)}) copy-start(bf16[512,1536]{1,0:T(8,128)(2,1)} %w_own.1) | copy-start | bytes 4718596
  2.0 18.6 %collective-permute-start.6 = (bf16[2,768,1536]{2,1,0:T(8,128)(2,1)}, bf16[2,768,1536]{2,1,0:T(8,128)(2,1)}, u32[]{:S(2)}, u32[]{:S(2)}) collective-permute-start(bf16[2,768,1536]{2,1,0:T(8,128)(2,1)} %mix_own.1), channel_id=1, source_target_pairs={{0,1},{1,0},{2,3},{3,2},{4,5},{5,4},{6,7},{7,6},{8,9},{9,8},{10,11... | collective-permute-start | bytes 14155784 | tf_op jit(solution)/shard_map/ppermute | solution.py:22
  2.4 16.1 %collective-permute-start.3 = (bf16[256,768]{1,0:T(8,128)(2,1)}, bf16[256,768]{1,0:T(8,128)(2,1)S(1)}, u32[]{:S(2)}, u32[]{:S(2)}) collective-permute-start(bf16[256,768]{1,0:T(8,128)(2,1)} %x_own.1), channel_id=1, source_target_pairs={{0,1},{1,0},{2,3},{3,2},{4,5},{5,4},{6,7},{7,6},{8,9},{9,8},{10,11... | collective-permute-start | bytes 1179656 | tf_op jit(solution)/shard_map/ppermute | solution.py:22
  2.5 16.0 %collective-permute-start = (bf16[192,768]{1,0:T(8,128)(2,1)}, bf16[192,768]{1,0:T(8,128)(2,1)S(1)}, u32[]{:S(2)}, u32[]{:S(2)}) collective-permute-start(bf16[192,768]{1,0:T(8,128)(2,1)} %get-tuple-element.40), channel_id=1, source_target_pairs={{0,2},{2,0},{4,6},{6,4},{8,10},{10,8},{12,14},{14,12},{1,3},{3,1},... | collective-permute-start | bytes 884744 | tf_op jit(solution)/shard_map/ppermute | solution.py:253
  5.4 13.1 %collective-permute-start.1 = (bf16[192,768]{1,0:T(8,128)(2,1)S(1)}, bf16[192,768]{1,0:T(8,128)(2,1)S(1)}, u32[]{:S(2)}, u32[]{:S(2)}) collective-permute-start(bf16[192,768]{1,0:T(8,128)(2,1)S(1)} %get-tuple-element.41), channel_id=1, source_target_pairs={{0,0},{14,14},{2,4},{4,2},{6,8},{8,6},{10,12},{12,10},{1,1},{15,15... | collective-permute-start | bytes 884744 | tf_op jit(solution)/shard_map/ppermute | solution.py:254
  8.4 2.2 %collective-permute-start.2 = (f32[16,768]{1,0:T(8,128)S(1)}, f32[16,768]{1,0:T(8,128)S(1)}, u32[]{:S(2)}, u32[]{:S(2)}) collective-permute-start(f32[16,768]{1,0:T(8,128)S(1)} %maximum_maximum_fusion.small_own), channel_id=1, source_target_pairs={{0,1},{1,0},{2,3},{3,2},{4,5},{5,4},{6,7},{7,6},{8,9},{9,8},{10,11... | collective-permute-start | bytes 147464 | tf_op jit(solution)/shard_map/ppermute | solution.py:22
  10.6 49.9 %collective-permute-start.16 = (bf16[512,1536]{1,0:T(8,128)(2,1)S(1)}, bf16[512,1536]{1,0:T(8,128)(2,1)S(1)}, u32[]{:S(2)}, u32[]{:S(2)}) collective-permute-start(bf16[512,1536]{1,0:T(8,128)(2,1)S(1)} %copy-done.2), channel_id=1, source_target_pairs={{0,1},{1,0},{2,3},{3,2},{4,5},{5,4},{6,7},{7,6},{8,9},{9,8},{10,11... | collective-permute-start | bytes 4718600 | tf_op jit(solution)/shard_map/ppermute | solution.py:22
  18.5 1.6 %collective-permute-start.4 = (bf16[192,768]{1,0:T(8,128)(2,1)S(1)}, bf16[192,768]{1,0:T(8,128)(2,1)S(1)}, u32[]{:S(2)}, u32[]{:S(2)}) collective-permute-start(bf16[192,768]{1,0:T(8,128)(2,1)S(1)} %collective-permute-done.near_own), channel_id=1, source_target_pairs={{0,1},{1,0},{2,3},{3,2},{4,5},{5,4},{6,7},{7,6},{8,9},{9,8},{10,11... | collective-permute-start | bytes 884744 | tf_op jit(solution)/shard_map/ppermute | solution.py:22
  18.5 2.0 %collective-permute-start.5 = (bf16[192,768]{1,0:T(8,128)(2,1)S(1)}, bf16[192,768]{1,0:T(8,128)(2,1)S(1)}, u32[]{:S(2)}, u32[]{:S(2)}) collective-permute-start(bf16[192,768]{1,0:T(8,128)(2,1)S(1)} %collective-permute-done.1.far_own), channel_id=1, source_target_pairs={{0,1},{1,0},{2,3},{3,2},{4,5},{5,4},{6,7},{7,6},{8,9},{9,8},{10,11... | collective-permute-start | bytes 884744 | tf_op jit(solution)/shard_map/ppermute | solution.py:22
  28.3 5.2 %copy-start.1 = (bf16[1536,512]{1,0:T(8,128)(2,1)S(1)}, bf16[1536,512]{1,0:T(8,128)(2,1)}, u32[]{:S(2)}) copy-start(bf16[1536,512]{1,0:T(8,128)(2,1)} %weight.1) | copy-start | bytes 4718596
  28.3 1.8 %collective-permute-start.7 = (bf16[128,1536]{1,0:T(8,128)(2,1)S(1)}, bf16[128,1536]{1,0:T(8,128)(2,1)S(1)}, u32[]{:S(2)}, u32[]{:S(2)}) collective-permute-start(bf16[128,1536]{1,0:T(8,128)(2,1)S(1)} %get-tuple-element.50.own_ref), channel_id=1, source_target_pairs={{0,1},{1,0},{2,3},{3,2},{4,5},{5,4},{6,7},{7,6},{8,9},{9,8},{10,11... | collective-permute-start | bytes 1179656 | tf_op jit(solution)/shard_map/ppermute | solution.py:22
  31.0 6.2 %collective-permute-start.8 = (bf16[256,256]{1,0:T(8,128)(2,1)S(1)}, bf16[256,256]{1,0:T(8,128)(2,1)S(1)}, u32[]{:S(2)}, u32[]{:S(2)}) collective-permute-start(bf16[256,256]{1,0:T(8,128)(2,1)S(1)} %keyvalue.1.refs_1_), channel_id=1, source_target_pairs={{0,4},{4,8},{8,12},{12,14},{14,10},{10,6},{6,2},{2,0},{1,5},{5,9},... | collective-permute-start | bytes 393224 | tf_op jit(solution)/shard_map/ppermute | solution.py:312
  33.5 5.3 %collective-permute-start.9 = (bf16[256,256]{1,0:T(8,128)(2,1)S(1)}, bf16[256,256]{1,0:T(8,128)(2,1)S(1)}, u32[]{:S(2)}, u32[]{:S(2)}) collective-permute-start(bf16[256,256]{1,0:T(8,128)(2,1)S(1)} %keyvalue.1.refs_1_), channel_id=1, source_target_pairs={{4,0},{8,4},{12,8},{14,12},{10,14},{6,10},{2,6},{0,2},{5,1},{9,5},... | collective-permute-start | bytes 393224 | tf_op jit(solution)/shard_map/ppermute | solution.py:315
  38.8 5.0 %collective-permute-start.10 = (bf16[256,256]{1,0:T(8,128)(2,1)S(1)}, bf16[256,256]{1,0:T(8,128)(2,1)S(1)}, u32[]{:S(2)}, u32[]{:S(2)}) collective-permute-start(bf16[256,256]{1,0:T(8,128)(2,1)S(1)} %collective-permute-done.8.refs_1_), channel_id=1, source_target_pairs={{0,4},{4,8},{8,12},{12,14},{14,10},{10,6},{6,2},{2,0},{1,5},{5,9},... | collective-permute-start | bytes 393224 | tf_op jit(solution)/shard_map/ppermute | solution.py:312
  40.3 5.0 %collective-permute-start.11 = (bf16[256,256]{1,0:T(8,128)(2,1)S(1)}, bf16[256,256]{1,0:T(8,128)(2,1)S(1)}, u32[]{:S(2)}, u32[]{:S(2)}) collective-permute-start(bf16[256,256]{1,0:T(8,128)(2,1)S(1)} %collective-permute-done.9.refs_2_), channel_id=1, source_target_pairs={{4,0},{8,4},{12,8},{14,12},{10,14},{6,10},{2,6},{0,2},{5,1},{9,5},... | collective-permute-start | bytes 393224 | tf_op jit(solution)/shard_map/ppermute | solution.py:315
  45.3 5.0 %collective-permute-start.12 = (bf16[256,256]{1,0:T(8,128)(2,1)S(1)}, bf16[256,256]{1,0:T(8,128)(2,1)S(1)}, u32[]{:S(2)}, u32[]{:S(2)}) collective-permute-start(bf16[256,256]{1,0:T(8,128)(2,1)S(1)} %collective-permute-done.10.refs_1_), channel_id=1, source_target_pairs={{0,4},{4,8},{8,12},{12,14},{14,10},{10,6},{6,2},{2,0},{1,5},{5,9},... | collective-permute-start | bytes 393224 | tf_op jit(solution)/shard_map/ppermute | solution.py:312
  46.9 5.0 %collective-permute-start.13 = (bf16[256,256]{1,0:T(8,128)(2,1)S(1)}, bf16[256,256]{1,0:T(8,128)(2,1)S(1)}, u32[]{:S(2)}, u32[]{:S(2)}) collective-permute-start(bf16[256,256]{1,0:T(8,128)(2,1)S(1)} %collective-permute-done.11.refs_2_), channel_id=1, source_target_pairs={{4,0},{8,4},{12,8},{14,12},{10,14},{6,10},{2,6},{0,2},{5,1},{9,5},... | collective-permute-start | bytes 393224 | tf_op jit(solution)/shard_map/ppermute | solution.py:315
  47.3 12.2 %collective-permute-start.17 = (f32[128,768]{1,0:T(8,128)S(1)}, f32[128,768]{1,0:T(8,128)S(1)}, u32[]{:S(2)}, u32[]{:S(2)}) collective-permute-start(f32[128,768]{1,0:T(8,128)S(1)} %get-tuple-element.74), channel_id=1, source_target_pairs={{0,1},{1,0},{2,3},{3,2},{4,5},{5,4},{6,7},{7,6},{8,9},{9,8},{10,11... | collective-permute-start | bytes 1179656 | tf_op jit(solution)/shard_map/ppermute | solution.py:22
  51.9 5.0 %collective-permute-start.14 = (bf16[256,256]{1,0:T(8,128)(2,1)S(1)}, bf16[256,256]{1,0:T(8,128)(2,1)S(1)}, u32[]{:S(2)}, u32[]{:S(2)}) collective-permute-start(bf16[256,256]{1,0:T(8,128)(2,1)S(1)} %collective-permute-done.12.refs_1_), channel_id=1, source_target_pairs={{0,4},{4,8},{8,12},{12,14},{14,10},{10,6},{6,2},{2,0},{1,5},{5,9},... | collective-permute-start | bytes 393224 | tf_op jit(solution)/shard_map/ppermute | solution.py:312
  59.4 1.6 %collective-permute-start.15 = (bf16[256,512]{1,0:T(8,128)(2,1)S(1)}, bf16[256,512]{1,0:T(8,128)(2,1)S(1)}, u32[]{:S(2)}, u32[]{:S(2)}) collective-permute-start(bf16[256,512]{1,0:T(8,128)(2,1)S(1)} %attend_last.1.ctx), channel_id=1, source_target_pairs={{0,1},{1,0},{2,3},{3,2},{4,5},{5,4},{6,7},{7,6},{8,9},{9,8},{10,11... | collective-permute-start | bytes 786440 | tf_op jit(solution)/shard_map/ppermute | solution.py:22

commit v3 on v2

--- a/solution.py
+++ b/solution.py
@@ -165,32 +165,34 @@
         cols = slice(head * HD, (head + 1) * HD)
         q = q_ref[:, cols]
         scores = [
-            lax.dot_general(q, kv[:, 0:HD], (((1,), (1,)), ((), ())), preferred_element_type=F32) for kv in blocks
+            lax.dot_general(kv[:, 0:HD], q, (((1,), (1,)), ((), ())), preferred_element_type=F32) for kv in blocks
         ]
-        peaks = [jnp.max(s, axis=1, keepdims=True) for s in scores]
+        peaks = [jnp.max(s, axis=0, keepdims=True) for s in scores]
         total = None
         context = None
         if not first:
             stats, summed = state_in
-            before = stats[:, head : head + 1]
+            before = stats[head : head + 1, :]
             peaks.append(before)
         peak = functools.reduce(jnp.maximum, peaks)
         if not first:
             keep = jnp.exp2((before - peak) * factor)
-            total = stats[:, heads + head : heads + head + 1] * keep
-            context = summed[:, cols] * keep
+            total = stats[heads + head : heads + head + 1, :] * keep
+            context = summed[cols, :] * keep
         for s, kv in zip(scores, blocks):
             probs = jnp.exp2((s - peak) * factor)
-            part = jnp.sum(probs, axis=1, keepdims=True)
-            value = jnp.dot(probs.astype(BF16), kv[:, HD:], preferred_element_type=F32)
+            part = jnp.sum(probs, axis=0, keepdims=True)
+            value = lax.dot_general(
+                kv[:, HD:], probs.astype(BF16), (((0,), (0,)), ((), ())), preferred_element_type=F32
+            )
             total = part if total is None else total + part
             context = value if context is None else context + value
         if last:
-            refs[0][:, cols] = (context / total).astype(BF16)
+            refs[0][:, cols] = jnp.transpose(context * (1.0 / total)).astype(BF16)
         else:
-            refs[0][:, head : head + 1] = peak
-            refs[0][:, heads + head : heads + head + 1] = total
-            refs[1][:, cols] = context
+            refs[0][head : head + 1, :] = peak
+            refs[0][heads + head : heads + head + 1, :] = total
+            refs[1][cols, :] = context
 
 
 def begin_kernel(place, ctx, w_own, hid_own, hid_peer, out):
@@ -319,13 +321,15 @@
             hidden_peer = peer(hidden_away)
         state = call(
             functools.partial(attend_kernel, count=len(fresh), scale=1.0 / math.sqrt(HD), first=step == 0, last=False),
-            [((rows, HD), F32), ((rows, heads * HD), F32)],
+            [((2 * heads, rows), F32), ((heads * HD, rows), F32)],
             "attend%d" % step,
             8,
             queries, *fresh, *state,
         )
         if step + 1 < size // 2:
-            up, down, *state = lax.optimization_barrier((up, down, *state))
+            up, *state = lax.optimization_barrier((up, *state))
+            if len(arrived) > 1:
+                down, *state = lax.optimization_barrier((down, *state))
             arrived = [up, down]
         fresh = arrived
     context = call(

time: 63 us -> 57.2 us (0.908)
  waiting for transfers between devices: 23.7 us -> 17.6 us
  starting transfers between devices: 12.2 us -> 13.6 us
  Pallas kernels: 21.1 us -> 19.9 us
    ppermute x3, waiting for transfers between devices: 4.68 us -> 0.95 us  [local(): down = lax.ppermute(down, 'seq', behind)]
    ppermute x4, waiting for transfers between devices: 7 us -> 4.63 us  [local(): up = lax.ppermute(up, 'seq', ahead)]
    ppermute x4, starting transfers between devices: 5.99 us -> 7.76 us  [local(): up = lax.ppermute(up, 'seq', ahead)]
    pallas_call x10, Pallas kernels: 21.1 us -> 19.9 us  [call(): pl.pallas_call(kernel, out_shape=shapes, in_specs=in_specs, out_specs=(VM...]
  transfers between devices with their start and end apart: 18 -> 18, of which waited for: 13 -> 11; matrix products, arithmetic and copies ran while one was open for 6% -> 6% of each run, Pallas kernels for 31% -> 32%
where the time goes in v3:
time: 57.2 us; the launch traced here: 56.9 us
  Pallas kernels  19.9 us (35%)
  waiting for transfers between devices  17.6 us (31%)
  starting transfers between devices  13.6 us (24%)
  local copies, waits for them, and re-layouts  2.79 us (5%)
  other arithmetic  2.79 us (5%)
    pallas_call x10, Pallas kernels, call(): pl.pallas_call(kernel, out_shape=shapes, in_specs=in_specs, out_specs=(VM...  19.9 us
    ppermute x4, starting transfers between devices, local(): up = lax.ppermute(up, 'seq', ahead)  7.76 us
    ppermute x1, waiting for transfers between devices, local(): near = lax.ppermute(to_near, 'seq', near_pairs)  7.47 us
    ppermute x4, waiting for transfers between devices, local(): up = lax.ppermute(up, 'seq', ahead)  4.63 us
    ppermute x9, waiting for transfers between devices, peer(): return lax.ppermute(array, 'ch', SWAP)  4.53 us
    ppermute x1, starting transfers between devices, local(): near = lax.ppermute(to_near, 'seq', near_pairs)  2.97 us
    unnamed x8, local copies, waits for them, and re-layouts  2.01 us
    select_n x1, other arithmetic, local(): jnp.where(even, low, high)  1.95 us
  transfers between devices with their start and end apart: 18, of which 11 were waited for; matrix products, arithmetic and copies ran while one was open for 6% of the time, Pallas kernels for 32%

profile of v3, /device:TPU:0, one launch (start us, length us, event | category | flops | bytes accessed | tf_op | source)
XLA Modules:
  0.0 56.9 jit_solution(18230003858090261089)
XLA Ops:
  0.0 1.9 %broadcast_select_fusion = (bf16[192,768]{1,0:T(8,128)(2,1)S(1)}, bf16[192,768]{1,0:T(8,128)(2,1)}) fusion(pred[]{:T(512)S(6)} %eq.5, bf16[256,768]{1,0:T(8,128)(2,1)} %x_own.1), kind=kLoop, calls=%fused_computation.1 | loop fusion | flops 294912 | bytes 1179649 | tf_op jit(solution)/shard_map/jit(_where)/select_n | solution.py:253
  2.5 3.0 %collective-permute-start = (bf16[192,768]{1,0:T(8,128)(2,1)}, bf16[192,768]{1,0:T(8,128)(2,1)S(1)}, u32[]{:S(2)}, u32[]{:S(2)}) collective-permute-start(bf16[192,768]{1,0:T(8,128)(2,1)} %get-tuple-element.46), channel_id=1, source_target_pairs={{0,2},{2,0},{4,6},{6,4},{8,10},{10,8},{12,14},{14,12},{1,3},{3,1},... | collective-permute-start | bytes 884744 | tf_op jit(solution)/shard_map/ppermute | solution.py:255
  8.4 1.2 %copy.13 = bf16[192,8,2,128]{3,1,2,0:T(8,128)(2,1)S(1)} copy(bf16[192,8,2,128]{3,2,1,0:T(2,128)(2,1)} %bitcast.9) | data formatting | bytes 1572864
  11.0 7.5 %collective-permute-done.near_own = bf16[192,768]{1,0:T(8,128)(2,1)S(1)} collective-permute-done((bf16[192,768]{1,0:T(8,128)(2,1)}, bf16[192,768]{1,0:T(8,128)(2,1)S(1)}, u32[]{:S(2)}, u32[]{:S(2)}) %collective-permute-start) | collective-permute-done | bytes 294944 | tf_op jit(solution)/shard_map/ppermute | solution.py:255
  19.0 1.1 %collective-permute-done.4.near_peer = bf16[192,768]{1,0:T(8,128)(2,1)S(1)} collective-permute-done((bf16[192,768]{1,0:T(8,128)(2,1)S(1)}, bf16[192,768]{1,0:T(8,128)(2,1)S(1)}, u32[]{:S(2)}, u32[]{:S(2)}) %collective-permute-start.4) | collective-permute-done | bytes 294944 | tf_op jit(solution)/shard_map/ppermute | solution.py:22
  20.5 7.8 %tower.1 = (bf16[128,1536]{1,0:T(8,128)(2,1)S(1)}, f32[128,768]{1,0:T(8,128)S(1)}, f32[128,768]{1,0:T(8,128)S(1)}) custom-call(s32[4]{0:T(128)S(1)} %pad_add_fusion.place, bf16[256,768]{1,0:T(8,128)(2,1)S(1)} %copy-done, bf16[256,768]{1,0:T(8,128)(2,1)S(1)} %collective-permute-done.3.x_peer, bf16[192,768]{1,0:T(8,128)(2,1)S(1)} %collective-permute-done.near_own, ...), custom_call_target="tpu_custom_call" | custom-call | tf_op jit(solution)/shard_map/tower/pallas_call | solution.py:221
  28.5 1.6 %collective-permute-done.7.peer_ref = bf16[128,1536]{1,0:T(8,128)(2,1)S(1)} collective-permute-done((bf16[128,1536]{1,0:T(8,128)(2,1)S(1)}, bf16[128,1536]{1,0:T(8,128)(2,1)S(1)}, u32[]{:S(2)}, u32[]{:S(2)}) %collective-permute-start.7) | collective-permute-done | bytes 393248 | tf_op jit(solution)/shard_map/ppermute | solution.py:22
  30.1 0.9 %keyvalue.1.refs_1_ = bf16[256,256]{1,0:T(8,128)(2,1)S(1)} custom-call(s32[4]{0:T(128)S(1)} %pad_add_fusion.place, bf16[128,1536]{1,0:T(8,128)(2,1)S(1)} %get-tuple-element.56.own_ref, bf16[128,1536]{1,0:T(8,128)(2,1)S(1)} %collective-permute-done.7.peer_ref, bf16[1536,256]{1,0:T(8,128)(2,1)S(1)} %bitcast.8), custom_call_target="tpu_custom_call" | custom-call | tf_op jit(solution)/shard_map/keyvalue/pallas_call | solution.py:221
  31.0 2.5 %collective-permute-start.8 = (bf16[256,256]{1,0:T(8,128)(2,1)S(1)}, bf16[256,256]{1,0:T(8,128)(2,1)S(1)}, u32[]{:S(2)}, u32[]{:S(2)}) collective-permute-start(bf16[256,256]{1,0:T(8,128)(2,1)S(1)} %keyvalue.1.refs_1_), channel_id=1, source_target_pairs={{0,4},{4,8},{8,12},{12,14},{14,10},{10,6},{6,2},{2,0},{1,5},{5,9},... | collective-permute-start | bytes 393224 | tf_op jit(solution)/shard_map/ppermute | solution.py:314
  33.5 1.1 %query.1.refs_0_ = bf16[256,512]{1,0:T(8,128)(2,1)S(1)} custom-call(s32[4]{0:T(128)S(1)} %pad_add_fusion.place, bf16[128,1536]{1,0:T(8,128)(2,1)S(1)} %get-tuple-element.56.own_ref, bf16[128,1536]{1,0:T(8,128)(2,1)S(1)} %collective-permute-done.7.peer_ref, bf16[1536,512]{1,0:T(8,128)(2,1)S(1)} %copy-done.1), custom_call_target="tpu_custom_call" | custom-call | tf_op jit(solution)/shard_map/query/pallas_call | solution.py:221
  34.7 1.3 %attend0.1 = (f32[8,256]{1,0:T(8,128)S(1)}, f32[512,256]{1,0:T(8,128)S(1)}) custom-call(bf16[256,512]{1,0:T(8,128)(2,1)S(1)} %query.1.refs_0_, bf16[256,256]{1,0:T(8,128)(2,1)S(1)} %keyvalue.1.refs_1_), custom_call_target="tpu_custom_call" | custom-call | tf_op jit(solution)/shard_map/attend0/pallas_call | solution.py:221
  36.0 1.3 %collective-permute-done.8.refs_1_ = bf16[256,256]{1,0:T(8,128)(2,1)S(1)} collective-permute-done((bf16[256,256]{1,0:T(8,128)(2,1)S(1)}, bf16[256,256]{1,0:T(8,128)(2,1)S(1)}, u32[]{:S(2)}, u32[]{:S(2)}) %collective-permute-start.8) | collective-permute-done | bytes 131104 | tf_op jit(solution)/shard_map/ppermute | solution.py:314
  37.3 1.8 %collective-permute-start.9 = (bf16[256,256]{1,0:T(8,128)(2,1)S(1)}, bf16[256,256]{1,0:T(8,128)(2,1)S(1)}, u32[]{:S(2)}, u32[]{:S(2)}) collective-permute-start(bf16[256,256]{1,0:T(8,128)(2,1)S(1)} %collective-permute-done.8.refs_1_), channel_id=1, source_target_pairs={{0,4},{4,8},{8,12},{12,14},{14,10},{10,6},{6,2},{2,0},{1,5},{5,9},... | collective-permute-start | bytes 393224 | tf_op jit(solution)/shard_map/ppermute | solution.py:314
  39.3 1.6 %attend1.1 = (f32[8,256]{1,0:T(8,128)S(1)}, f32[512,256]{1,0:T(8,128)S(1)}) custom-call(bf16[256,512]{1,0:T(8,128)(2,1)S(1)} %query.1.refs_0_, bf16[256,256]{1,0:T(8,128)(2,1)S(1)} %collective-permute-done.8.refs_1_, bf16[256,256]{1,0:T(8,128)(2,1)S(1)} %collective-permute-done.10.refs_2_, f32[8,256]{1,0:T(8,128)S(1)} %get-tuple-element.64.refs_3_, ...), custom_call_target="tpu_custom_call" | custom-call | tf_op jit(solution)/shard_map/attend1/pallas_call | solution.py:221
  40.9 1.4 %collective-permute-done.9.refs_1_ = bf16[256,256]{1,0:T(8,128)(2,1)S(1)} collective-permute-done((bf16[256,256]{1,0:T(8,128)(2,1)S(1)}, bf16[256,256]{1,0:T(8,128)(2,1)S(1)}, u32[]{:S(2)}, u32[]{:S(2)}) %collective-permute-start.9) | collective-permute-done | bytes 131104 | tf_op jit(solution)/shard_map/ppermute | solution.py:314
  42.3 1.7 %collective-permute-start.11 = (bf16[256,256]{1,0:T(8,128)(2,1)S(1)}, bf16[256,256]{1,0:T(8,128)(2,1)S(1)}, u32[]{:S(2)}, u32[]{:S(2)}) collective-permute-start(bf16[256,256]{1,0:T(8,128)(2,1)S(1)} %collective-permute-done.9.refs_1_), channel_id=1, source_target_pairs={{0,4},{4,8},{8,12},{12,14},{14,10},{10,6},{6,2},{2,0},{1,5},{5,9},... | collective-permute-start | bytes 393224 | tf_op jit(solution)/shard_map/ppermute | solution.py:314
  44.3 1.6 %attend2.1 = (f32[8,256]{1,0:T(8,128)S(1)}, f32[512,256]{1,0:T(8,128)S(1)}) custom-call(bf16[256,512]{1,0:T(8,128)(2,1)S(1)} %query.1.refs_0_, bf16[256,256]{1,0:T(8,128)(2,1)S(1)} %collective-permute-done.9.refs_1_, bf16[256,256]{1,0:T(8,128)(2,1)S(1)} %collective-permute-done.12.refs_2_, f32[8,256]{1,0:T(8,128)S(1)} %get-tuple-element.72.refs_3_, ...), custom_call_target="tpu_custom_call" | custom-call | tf_op jit(solution)/shard_map/attend2/pallas_call | solution.py:221
  45.9 1.3 %collective-permute-done.11.refs_1_ = bf16[256,256]{1,0:T(8,128)(2,1)S(1)} collective-permute-done((bf16[256,256]{1,0:T(8,128)(2,1)S(1)}, bf16[256,256]{1,0:T(8,128)(2,1)S(1)}, u32[]{:S(2)}, u32[]{:S(2)}) %collective-permute-start.11) | collective-permute-done | bytes 131104 | tf_op jit(solution)/shard_map/ppermute | solution.py:314
  47.3 1.7 %collective-permute-start.13 = (bf16[256,256]{1,0:T(8,128)(2,1)S(1)}, bf16[256,256]{1,0:T(8,128)(2,1)S(1)}, u32[]{:S(2)}, u32[]{:S(2)}) collective-permute-start(bf16[256,256]{1,0:T(8,128)(2,1)S(1)} %collective-permute-done.11.refs_1_), channel_id=1, source_target_pairs={{0,4},{4,8},{8,12},{12,14},{14,10},{10,6},{6,2},{2,0},{1,5},{5,9},... | collective-permute-start | bytes 393224 | tf_op jit(solution)/shard_map/ppermute | solution.py:314
  49.0 0.9 %collective-permute-done.14.refs_2_ = bf16[256,256]{1,0:T(8,128)(2,1)S(1)} collective-permute-done((bf16[256,256]{1,0:T(8,128)(2,1)S(1)}, bf16[256,256]{1,0:T(8,128)(2,1)S(1)}, u32[]{:S(2)}, u32[]{:S(2)}) %collective-permute-start.14) | collective-permute-done | bytes 131104 | tf_op jit(solution)/shard_map/ppermute | solution.py:317
  49.9 1.6 %attend3.1 = (f32[8,256]{1,0:T(8,128)S(1)}, f32[512,256]{1,0:T(8,128)S(1)}) custom-call(bf16[256,512]{1,0:T(8,128)(2,1)S(1)} %query.1.refs_0_, bf16[256,256]{1,0:T(8,128)(2,1)S(1)} %collective-permute-done.11.refs_1_, bf16[256,256]{1,0:T(8,128)(2,1)S(1)} %collective-permute-done.14.refs_2_, f32[8,256]{1,0:T(8,128)S(1)} %get-tuple-element.80.refs_3_, ...), custom_call_target="tpu_custom_call" | custom-call | tf_op jit(solution)/shard_map/attend3/pallas_call | solution.py:221
  52.2 1.4 %attend_last.1.ctx = bf16[256,512]{1,0:T(8,128)(2,1)S(1)} custom-call(bf16[256,512]{1,0:T(8,128)(2,1)S(1)} %query.1.refs_0_, bf16[256,256]{1,0:T(8,128)(2,1)S(1)} %collective-permute-done.13.refs_1_, f32[8,256]{1,0:T(8,128)S(1)} %get-tuple-element.82.refs_2_, f32[512,256]{1,0:T(8,128)S(1)} %get-tuple-element.83.refs_3_), custom_call_target="tpu_custom_call" | custom-call | tf_op jit(solution)/shard_map/attend_last/pallas_call | solution.py:221
  53.7 0.9 %begin.1.partial = f32[256,768]{1,0:T(8,128)S(1)} custom-call(s32[4]{0:T(128)S(1)} %pad_add_fusion.place, bf16[256,512]{1,0:T(8,128)(2,1)S(1)} %attend_last.1.ctx, bf16[512,1536]{1,0:T(8,128)(2,1)S(1)} %copy-done.2, f32[128,768]{1,0:T(8,128)S(1)} %get-tuple-element.85.hid_own, f32[128,768]{1,0:T(8,128)S(1)} %collective-permute-done.17.hid_peer), custom_call_target="tpu_custom_call" | custom-call | tf_op jit(solution)/shard_map/begin/pallas_call | solution.py:221
  55.2 1.7 %finish.1 = bf16[256,768]{1,0:T(8,128)(2,1)} custom-call(s32[4]{0:T(128)S(1)} %pad_add_fusion.place, bf16[256,512]{1,0:T(8,128)(2,1)S(1)} %collective-permute-done.15.ctx, bf16[512,1536]{1,0:T(8,128)(2,1)S(1)} %collective-permute-done.16.w_peer, f32[256,768]{1,0:T(8,128)S(1)} %begin.1.partial), custom_call_target="tpu_custom_call" | custom-call | tf_op jit(solution)/shard_map/finish/pallas_call | solution.py:221
  (37 shorter events, 7.8 us)
Async XLA Ops:
  0.0 20.5 %copy-start = (bf16[256,768]{1,0:T(8,128)(2,1)S(1)}, bf16[256,768]{1,0:T(8,128)(2,1)}, u32[]{:S(2)}) copy-start(bf16[256,768]{1,0:T(8,128)(2,1)} %x_own.1) | copy-start | bytes 1179652
  0.0 10.6 %copy-start.2 = (bf16[512,1536]{1,0:T(8,128)(2,1)S(1)}, bf16[512,1536]{1,0:T(8,128)(2,1)}, u32[]{:S(2)}) copy-start(bf16[512,1536]{1,0:T(8,128)(2,1)} %w_own.1) | copy-start | bytes 4718596
  2.0 18.6 %collective-permute-start.6 = (bf16[2,768,1536]{2,1,0:T(8,128)(2,1)}, bf16[2,768,1536]{2,1,0:T(8,128)(2,1)}, u32[]{:S(2)}, u32[]{:S(2)}) collective-permute-start(bf16[2,768,1536]{2,1,0:T(8,128)(2,1)} %mix_own.1), channel_id=1, source_target_pairs={{0,1},{1,0},{2,3},{3,2},{4,5},{5,4},{6,7},{7,6},{8,9},{9,8},{10,11... | collective-permute-start | bytes 14155784 | tf_op jit(solution)/shard_map/ppermute | solution.py:22
  2.4 16.1 %collective-permute-start.3 = (bf16[256,768]{1,0:T(8,128)(2,1)}, bf16[256,768]{1,0:T(8,128)(2,1)S(1)}, u32[]{:S(2)}, u32[]{:S(2)}) collective-permute-start(bf16[256,768]{1,0:T(8,128)(2,1)} %x_own.1), channel_id=1, source_target_pairs={{0,1},{1,0},{2,3},{3,2},{4,5},{5,4},{6,7},{7,6},{8,9},{9,8},{10,11... | collective-permute-start | bytes 1179656 | tf_op jit(solution)/shard_map/ppermute | solution.py:22
  2.5 16.0 %collective-permute-start = (bf16[192,768]{1,0:T(8,128)(2,1)}, bf16[192,768]{1,0:T(8,128)(2,1)S(1)}, u32[]{:S(2)}, u32[]{:S(2)}) collective-permute-start(bf16[192,768]{1,0:T(8,128)(2,1)} %get-tuple-element.46), channel_id=1, source_target_pairs={{0,2},{2,0},{4,6},{6,4},{8,10},{10,8},{12,14},{14,12},{1,3},{3,1},... | collective-permute-start | bytes 884744 | tf_op jit(solution)/shard_map/ppermute | solution.py:255
  5.4 13.1 %collective-permute-start.1 = (bf16[192,768]{1,0:T(8,128)(2,1)S(1)}, bf16[192,768]{1,0:T(8,128)(2,1)S(1)}, u32[]{:S(2)}, u32[]{:S(2)}) collective-permute-start(bf16[192,768]{1,0:T(8,128)(2,1)S(1)} %get-tuple-element.47), channel_id=1, source_target_pairs={{0,0},{14,14},{2,4},{4,2},{6,8},{8,6},{10,12},{12,10},{1,1},{15,15... | collective-permute-start | bytes 884744 | tf_op jit(solution)/shard_map/ppermute | solution.py:256
  8.4 2.2 %collective-permute-start.2 = (f32[16,768]{1,0:T(8,128)S(1)}, f32[16,768]{1,0:T(8,128)S(1)}, u32[]{:S(2)}, u32[]{:S(2)}) collective-permute-start(f32[16,768]{1,0:T(8,128)S(1)} %maximum_maximum_fusion.small_own), channel_id=1, source_target_pairs={{0,1},{1,0},{2,3},{3,2},{4,5},{5,4},{6,7},{7,6},{8,9},{9,8},{10,11... | collective-permute-start | bytes 147464 | tf_op jit(solution)/shard_map/ppermute | solution.py:22
  10.6 44.1 %collective-permute-start.16 = (bf16[512,1536]{1,0:T(8,128)(2,1)S(1)}, bf16[512,1536]{1,0:T(8,128)(2,1)S(1)}, u32[]{:S(2)}, u32[]{:S(2)}) collective-permute-start(bf16[512,1536]{1,0:T(8,128)(2,1)S(1)} %copy-done.2), channel_id=1, source_target_pairs={{0,1},{1,0},{2,3},{3,2},{4,5},{5,4},{6,7},{7,6},{8,9},{9,8},{10,11... | collective-permute-start | bytes 4718600 | tf_op jit(solution)/shard_map/ppermute | solution.py:22
  18.5 1.6 %collective-permute-start.4 = (bf16[192,768]{1,0:T(8,128)(2,1)S(1)}, bf16[192,768]{1,0:T(8,128)(2,1)S(1)}, u32[]{:S(2)}, u32[]{:S(2)}) collective-permute-start(bf16[192,768]{1,0:T(8,128)(2,1)S(1)} %collective-permute-done.near_own), channel_id=1, source_target_pairs={{0,1},{1,0},{2,3},{3,2},{4,5},{5,4},{6,7},{7,6},{8,9},{9,8},{10,11... | collective-permute-start | bytes 884744 | tf_op jit(solution)/shard_map/ppermute | solution.py:22
  18.5 2.0 %collective-permute-start.5 = (bf16[192,768]{1,0:T(8,128)(2,1)S(1)}, bf16[192,768]{1,0:T(8,128)(2,1)S(1)}, u32[]{:S(2)}, u32[]{:S(2)}) collective-permute-start(bf16[192,768]{1,0:T(8,128)(2,1)S(1)} %collective-permute-done.1.far_own), channel_id=1, source_target_pairs={{0,1},{1,0},{2,3},{3,2},{4,5},{5,4},{6,7},{7,6},{8,9},{9,8},{10,11... | collective-permute-start | bytes 884744 | tf_op jit(solution)/shard_map/ppermute | solution.py:22
  28.3 5.2 %copy-start.1 = (bf16[1536,512]{1,0:T(8,128)(2,1)S(1)}, bf16[1536,512]{1,0:T(8,128)(2,1)}, u32[]{:S(2)}) copy-start(bf16[1536,512]{1,0:T(8,128)(2,1)} %weight.1) | copy-start | bytes 4718596
  28.3 1.8 %collective-permute-start.7 = (bf16[128,1536]{1,0:T(8,128)(2,1)S(1)}, bf16[128,1536]{1,0:T(8,128)(2,1)S(1)}, u32[]{:S(2)}, u32[]{:S(2)}) collective-permute-start(bf16[128,1536]{1,0:T(8,128)(2,1)S(1)} %get-tuple-element.56.own_ref), channel_id=1, source_target_pairs={{0,1},{1,0},{2,3},{3,2},{4,5},{5,4},{6,7},{7,6},{8,9},{9,8},{10,11... | collective-permute-start | bytes 1179656 | tf_op jit(solution)/shard_map/ppermute | solution.py:22
  31.0 6.2 %collective-permute-start.8 = (bf16[256,256]{1,0:T(8,128)(2,1)S(1)}, bf16[256,256]{1,0:T(8,128)(2,1)S(1)}, u32[]{:S(2)}, u32[]{:S(2)}) collective-permute-start(bf16[256,256]{1,0:T(8,128)(2,1)S(1)} %keyvalue.1.refs_1_), channel_id=1, source_target_pairs={{0,4},{4,8},{8,12},{12,14},{14,10},{10,6},{6,2},{2,0},{1,5},{5,9},... | collective-permute-start | bytes 393224 | tf_op jit(solution)/shard_map/ppermute | solution.py:314
  33.5 5.6 %collective-permute-start.10 = (bf16[256,256]{1,0:T(8,128)(2,1)S(1)}, bf16[256,256]{1,0:T(8,128)(2,1)S(1)}, u32[]{:S(2)}, u32[]{:S(2)}) collective-permute-start(bf16[256,256]{1,0:T(8,128)(2,1)S(1)} %keyvalue.1.refs_1_), channel_id=1, source_target_pairs={{4,0},{8,4},{12,8},{14,12},{10,14},{6,10},{2,6},{0,2},{5,1},{9,5},... | collective-permute-start | bytes 393224 | tf_op jit(solution)/shard_map/ppermute | solution.py:317
  37.3 5.0 %collective-permute-start.9 = (bf16[256,256]{1,0:T(8,128)(2,1)S(1)}, bf16[256,256]{1,0:T(8,128)(2,1)S(1)}, u32[]{:S(2)}, u32[]{:S(2)}) collective-permute-start(bf16[256,256]{1,0:T(8,128)(2,1)S(1)} %collective-permute-done.8.refs_1_), channel_id=1, source_target_pairs={{0,4},{4,8},{8,12},{12,14},{14,10},{10,6},{6,2},{2,0},{1,5},{5,9},... | collective-permute-start | bytes 393224 | tf_op jit(solution)/shard_map/ppermute | solution.py:314
  39.1 5.0 %collective-permute-start.12 = (bf16[256,256]{1,0:T(8,128)(2,1)S(1)}, bf16[256,256]{1,0:T(8,128)(2,1)S(1)}, u32[]{:S(2)}, u32[]{:S(2)}) collective-permute-start(bf16[256,256]{1,0:T(8,128)(2,1)S(1)} %collective-permute-done.10.refs_2_), channel_id=1, source_target_pairs={{4,0},{8,4},{12,8},{14,12},{10,14},{6,10},{2,6},{0,2},{5,1},{9,5},... | collective-permute-start | bytes 393224 | tf_op jit(solution)/shard_map/ppermute | solution.py:317
  42.3 5.0 %collective-permute-start.11 = (bf16[256,256]{1,0:T(8,128)(2,1)S(1)}, bf16[256,256]{1,0:T(8,128)(2,1)S(1)}, u32[]{:S(2)}, u32[]{:S(2)}) collective-permute-start(bf16[256,256]{1,0:T(8,128)(2,1)S(1)} %collective-permute-done.9.refs_1_), channel_id=1, source_target_pairs={{0,4},{4,8},{8,12},{12,14},{14,10},{10,6},{6,2},{2,0},{1,5},{5,9},... | collective-permute-start | bytes 393224 | tf_op jit(solution)/shard_map/ppermute | solution.py:314
  44.0 9.7 %collective-permute-start.17 = (f32[128,768]{1,0:T(8,128)S(1)}, f32[128,768]{1,0:T(8,128)S(1)}, u32[]{:S(2)}, u32[]{:S(2)}) collective-permute-start(f32[128,768]{1,0:T(8,128)S(1)} %get-tuple-element.86), channel_id=1, source_target_pairs={{0,1},{1,0},{2,3},{3,2},{4,5},{5,4},{6,7},{7,6},{8,9},{9,8},{10,11... | collective-permute-start | bytes 1179656 | tf_op jit(solution)/shard_map/ppermute | solution.py:22
  44.0 5.9 %collective-permute-start.14 = (bf16[256,256]{1,0:T(8,128)(2,1)S(1)}, bf16[256,256]{1,0:T(8,128)(2,1)S(1)}, u32[]{:S(2)}, u32[]{:S(2)}) collective-permute-start(bf16[256,256]{1,0:T(8,128)(2,1)S(1)} %collective-permute-done.12.refs_2_), channel_id=1, source_target_pairs={{4,0},{8,4},{12,8},{14,12},{10,14},{6,10},{2,6},{0,2},{5,1},{9,5},... | collective-permute-start | bytes 393224 | tf_op jit(solution)/shard_map/ppermute | solution.py:317
  47.3 5.0 %collective-permute-start.13 = (bf16[256,256]{1,0:T(8,128)(2,1)S(1)}, bf16[256,256]{1,0:T(8,128)(2,1)S(1)}, u32[]{:S(2)}, u32[]{:S(2)}) collective-permute-start(bf16[256,256]{1,0:T(8,128)(2,1)S(1)} %collective-permute-done.11.refs_1_), channel_id=1, source_target_pairs={{0,4},{4,8},{8,12},{12,14},{14,10},{10,6},{6,2},{2,0},{1,5},{5,9},... | collective-permute-start | bytes 393224 | tf_op jit(solution)/shard_map/ppermute | solution.py:314
  53.6 1.6 %collective-permute-start.15 = (bf16[256,512]{1,0:T(8,128)(2,1)S(1)}, bf16[256,512]{1,0:T(8,128)(2,1)S(1)}, u32[]{:S(2)}, u32[]{:S(2)}) collective-permute-start(bf16[256,512]{1,0:T(8,128)(2,1)S(1)} %attend_last.1.ctx), channel_id=1, source_target_pairs={{0,1},{1,0},{2,3},{3,2},{4,5},{5,4},{6,7},{7,6},{8,9},{9,8},{10,11... | collective-permute-start | bytes 786440 | tf_op jit(solution)/shard_map/ppermute | solution.py:22
